TPU v7x, 256 devices: a whole 4x4x8 slice. The times are simulated.
256 devices in a mesh: row: 32 (over z, y_hi, core), col: 8 (over y_lo, x).
Axes of the slice: x: 4, y: 4 (y_hi: 2, y_lo: 2; y = y_hi * 2 + y_lo), z: 8, core: 2. Of those that a mesh axis runs over, the one named last changes fastest.
Arguments:
- samples: float32 [512, 16384], P(None, 'col'), may hold values from -0.8 to 0.8
- values: float32 [16384, 16384], P('row', 'col'), may hold values from -6 to 6
- diag_entries: float32 [16384], P('row'), may hold values from 16 to 32
- block_mask: int32 [64, 64], replicated, may hold values 0 or 1
Outputs:
- updated: float32 [16384, 16384], P('row', 'col')
All inputs are finite; a program needn't handle non-finite values.
Results may differ from a plain program's by a relative error of at most 0.0003.
Values sent between devices are 32-bit elements; how exact they have to be, the bound alone decides.
No kernel may reach another device: no remote copies, remote signals or barrier semaphores. Data moves between devices by JAX's collectives and lax.ppermute only.
A program may use at most 64 MiB of HBM per device.

v0:
```python
import functools
import itertools

import jax
import jax.numpy as jnp
from jax import lax
from jax.experimental import pallas as pl
from jax.experimental.pallas import tpu as pltpu
from jax.sharding import Mesh
from jax.sharding import PartitionSpec as P

ROW = ("z", "yh", "core")
COL = ("yl", "x")
ALL = ROW + COL
SIZES = (8, 2, 2, 2, 4)
Z = SIZES[0]

step_size = 8.0
penalty = 0.05


def moved(array, target):
    def place(z, yh, core, col):
        return ((z * 2 + yh) * 2 + core) * 8 + col

    everyone = itertools.product(range(8), range(2), range(2), range(8))
    return lax.ppermute(array, ALL, [(place(*at), place(*target(*at))) for at in everyone])


def swapped(array):
    return moved(array, lambda z, yh, core, col: (col, yh, core, z ^ col))


def up(array):
    return moved(array, lambda z, yh, core, col: ((z + 1) % Z, yh, core, col))


def down(array):
    return moved(array, lambda z, yh, core, col: ((z - 1) % Z, yh, core, col))


def both_ways(rising, falling):
    rising, falling = together(rising, falling)
    return together(up(rising), down(falling))


def together(*arrays):
    return lax.optimization_barrier(arrays)


def other_core(array):
    return moved(array, lambda z, yh, core, col: (z, yh, 1 - core, col))


def other_half(array):
    return moved(array, lambda z, yh, core, col: (z, 1 - yh, core, col))


LANES = 512


def in_hbm(array):
    return pltpu.with_memory_space_constraint(array, pltpu.HBM)


def split_in_two(array):
    high = array.astype(jnp.bfloat16)
    return high, (array - high.astype(jnp.float32)).astype(jnp.bfloat16)


def in_three(left, right):
    made = jnp.dot(left[1], right[0], preferred_element_type=jnp.float32)
    made += jnp.dot(left[0], right[1], preferred_element_type=jnp.float32)
    return made + jnp.dot(left[0], right[0], preferred_element_type=jnp.float32)


def dot(left, right):
    return jnp.dot(
        left, right, precision=lax.Precision.HIGH, preferred_element_type=jnp.float32
    )


def product_kernel(scale, sizes, at, *refs):
    xs, refs = refs[: sizes[0]], refs[sizes[0] :]
    others, refs = refs[: sizes[1]], refs[sizes[1] :]
    ys, samples, refs = refs[:2], refs[2], refs[3:]
    *final, out, high, low = refs
    step = pl.program_id(0)
    piece_rows = xs[0].shape[0]
    half = piece_rows // 2

    @pl.when(step == 0)
    def _():
        rows = []
        for which in (at[1], 1 - at[1]):
            rows += [x[pl.ds(pl.multiple_of(which * half, half), half), :] for x in xs]
        rows += [other[...] for other in others]
        high[...], low[...] = split_in_two(jnp.concatenate(rows).T)

    right = [y[...] for y in ys]
    for i in range(high.shape[1] // piece_rows - len(xs)):
        first = pl.multiple_of(at[2 + i] * piece_rows, piece_rows)
        right.append(samples[pl.ds(first, piece_rows), :])
    made = in_three((high[...], low[...]), split_in_two(jnp.concatenate(right)))
    if scale is None:
        out[...] = made
        return
    addend, omega, diag = final
    made = made + addend[...]
    behind = at[0] - step * LANES
    rows = lax.broadcasted_iota(jnp.int32, made.shape, 0)
    cols = lax.broadcasted_iota(jnp.int32, made.shape, 1)
    on_diag = cols - rows == behind
    gradient = made * scale - jnp.where(on_diag, 1.0 / diag[...], jnp.float32(0.0))
    stepped = omega[...] - step_size * gradient
    limit = step_size * penalty
    out[...] = jnp.where(on_diag, stepped, stepped - jnp.clip(stepped, -limit, limit))


def product(at, xs, others, ys, samples, scale=None, final=()):
    depth = sum(part.shape[0] for part in (*xs, *others))
    rows, cols = xs[0].shape[1], samples.shape[1]

    def whole(array):
        return pl.BlockSpec(array.shape, lambda j, *_: (0, 0))

    def tile(array):
        return pl.BlockSpec((array.shape[0], LANES), lambda j, *_: (0, j))

    xs, samples = [in_hbm(x) for x in xs], in_hbm(samples)
    if final:
        final = [in_hbm(final[0]), in_hbm(final[1]), final[2]]
    specs = [whole(part) for part in (*xs, *others)] + [tile(part) for part in (*ys, samples)]
    specs += [whole(part) if part.shape[1] == 1 else tile(part) for part in final]
    return pl.pallas_call(
        functools.partial(product_kernel, scale, (len(xs), len(others))),
        grid_spec=pltpu.PrefetchScalarGridSpec(
            num_scalar_prefetch=1,
            grid=(cols // LANES,),
            in_specs=specs,
            out_specs=pl.BlockSpec((rows, LANES), lambda j, *_: (0, j)),
            scratch_shapes=[pltpu.VMEM((rows, depth), jnp.bfloat16)] * 2,
        ),
        out_shape=pltpu.HBM((rows, cols), jnp.float32),
        cost_estimate=pl.CostEstimate(
            flops=6 * depth * rows * cols,
            bytes_accessed=4 * (depth * rows + depth * cols + (1 + len(final)) * rows * cols),
            transcendentals=0,
        ),
        compiler_params=pltpu.CompilerParams(vmem_limit_bytes=16 << 20),
        name="product",
    )(at, *xs, *others, *ys, samples, *final)


NEXT = (3, -3)
LATE = (2, -2, 1, -1, 0)
NEAR = (0, 1, -1, 2)
FAR = (-2, 3, -3, 4)


def per_device(samples, values, diag_entries, block_mask):
    tile_rows, tile_cols = values.shape
    sample_count = samples.shape[0]
    piece_rows = sample_count // Z
    half_rows = piece_rows // 2
    cut = half_rows // 2
    z, yh, core = (lax.axis_index(name) for name in ROW)
    col = lax.axis_index(COL)
    row_index = lax.axis_index(ROW)

    mine = lax.dynamic_slice(
        samples,
        ((z ^ 4) * piece_rows, (yh * 2 + core) * tile_rows),
        (piece_rows, tile_rows),
    )
    first = swapped(mine)

    def piece_of(d):
        return moved(
            first, lambda z, yh, core, col: (z, yh, core, (z ^ 4) ^ ((z + d) % Z) ^ col)
        )

    pieces = {4: first}
    pieces[3], pieces[-3], first = together(piece_of(3), piece_of(-3), first)
    pieces.update({d: piece_of(d) for d in LATE})

    mask_block = samples.shape[1] * lax.axis_size(COL) // block_mask.shape[0]
    mask_rows = tile_rows // mask_block
    mask_cols = tile_cols // mask_block
    tile_mask = lax.dynamic_slice(
        block_mask, (row_index * mask_rows, col * mask_cols), (mask_rows, mask_cols)
    )
    mask_lines = jnp.repeat(tile_mask.astype(jnp.float32), mask_block, axis=1)
    expanded = jnp.broadcast_to(
        mask_lines[:, None, :], (mask_rows, mask_block, tile_cols)
    ).reshape(tile_rows, tile_cols)
    row_ids = row_index * tile_rows + jnp.arange(tile_rows, dtype=jnp.int32)
    col_ids = col * tile_cols + jnp.arange(tile_cols, dtype=jnp.int32)
    on_diag = row_ids[:, None] == col_ids[None, :]
    omega = jnp.where(on_diag, diag_entries[:, None], expanded * values)

    def parts_of(order, sources):
        made = dot(jnp.concatenate([sources[d] for d in order]), omega)
        made = made.reshape(len(order), 2, half_rows, tile_cols)
        own = lax.dynamic_slice_in_dim(made, core, 1, 1)
        other = lax.dynamic_slice_in_dim(made, 1 - core, 1, 1)
        both = own + other_core(other)
        return {d: both[i, 0] for i, d in enumerate(order)}

    part = parts_of((4,), pieces)
    rising, falling = both_ways(part[4][:cut], part[4][cut:])
    part.update(parts_of(NEXT, pieces))
    rising = part[3] + jnp.concatenate([rising, jnp.zeros_like(rising)])
    falling = part[-3] + jnp.concatenate([jnp.zeros_like(falling), falling])
    rising, falling = both_ways(rising, falling)
    part.update(parts_of(LATE, pieces))
    rising, falling = both_ways(part[2] + rising, part[-2] + falling)
    rising, falling = part[1] + rising, part[-1] + falling
    rising, falling = both_ways(rising, falling)
    summed = part[0] + rising + falling
    summed = summed + other_half(summed)

    whole = {0: summed}
    wanted = lax.dynamic_slice_in_dim(summed, yh * 2 * tile_rows, 2 * tile_rows, 1)
    rising, falling, wanted = together(summed, summed, wanted)
    whole[-1], whole[1] = together(up(rising), down(falling))
    arrived = swapped(wanted)
    whole[-2], whole[2] = together(up(whole[-1]), down(whole[1]))
    kept = lax.dynamic_slice_in_dim(arrived, core * tile_rows, tile_rows, 1)
    given = lax.dynamic_slice_in_dim(arrived, (1 - core) * tile_rows, tile_rows, 1)
    given = other_core(given)
    zero = jnp.int32(0)
    piece = jnp.zeros((2, half_rows, tile_rows), jnp.float32)
    piece = lax.dynamic_update_slice(piece, kept[None], (core, zero, zero))
    piece = lax.dynamic_update_slice(piece, given[None], (1 - core, zero, zero))
    piece = piece.reshape(piece_rows, tile_rows)
    facing = moved(piece, lambda z, yh, core, col: (z, yh, core, col ^ 4))
    near_y = jnp.concatenate([whole[d] for d in NEAR])
    pair = jnp.concatenate([piece, facing])

    def along_x(array, by):
        return moved(
            array, lambda z, yh, core, col: (z, yh, core, col // 4 * 4 + (col % 4 + by) % 4)
        )

    whole[-3], whole[3] = together(up(whole[-2]), down(whole[2]))
    before, after = along_x(pair, 1), along_x(pair, -1)
    other_near_y = other_core(near_y)
    offset = row_index * tile_rows - col * tile_cols
    x_at, side = col % 4, col // 4
    match = [
        flip * 4 + (x_at + by) % 4 for by in (0, -1, 1, 2) for flip in (side, 1 - side)
    ]
    rising, falling = up(whole[-3][:cut]), down(whole[3][cut:])
    before, after, pair = together(before, after, pair)
    opposite = along_x(pair, 2)
    products = product(
        jnp.stack([offset, core, *match[:4]]),
        [pieces[d] for d in NEAR],
        [pair, before],
        [near_y, other_near_y],
        samples,
    )
    far_y = jnp.concatenate([whole[d] for d in FAR[:-1]] + [rising, falling])
    other_far_y = other_core(far_y)
    return product(
        jnp.stack([offset, core, *match[4:]]),
        [pieces[d] for d in FAR],
        [after, opposite],
        [far_y, other_far_y],
        samples,
        0.5 / sample_count,
        [products, omega, diag_entries[:, None]],
    )


def solution(mesh):
    split = Mesh(mesh.devices.reshape(SIZES), ALL)

    return jax.shard_map(
        per_device,
        mesh=split,
        in_specs=(P(None, COL), P(ROW, COL), P(ROW), P()),
        out_specs=P(ROW, COL),
        check_vma=False,
    )
```

profile of v0, /device:TPU:32, one launch (start us, length us, event | category | flops | bytes accessed | tf_op | source)
XLA Modules:
  0.0 168.9 jit_solution(5768407627113475206)
XLA Ops:
  0.9 2.9 %collective-permute-start = (f32[64,512]{1,0:T(8,128)S(1)}, f32[64,512]{1,0:T(8,128)S(1)}, u32[]{:S(2)}, u32[]{:S(2)}) collective-permute-start(f32[64,512]{1,0:T(8,128)S(1)} %dynamic_slice.33), channel_id=1, source_target_pairs={{0,0},{1,33},{2,66},{3,99},{4,132},{5,165},{6,198},{7,231},{8,8},{... | collective-permute-start | bytes 393224 | tf_op jit(solution)/shard_map/ppermute | solution.py:27
  4.8 2.7 %fusion.refs_10_ = f32[512,2048]{1,0:T(8,128)S(1)} fusion(f32[512,2048]{1,0:T(8,128)} %param.5, f32[2,2048]{1,0:T(2,128)S(1)} %bitcast.73, f32[512]{0:T(512)} %param.6, s32[2048]{0:T(1024)S(1)} %iota_add_fusion, s32[512]{0:T(512)S(1)} %iota_add_fusion.1), kind=kLoop, calls=%fused_computation.1 | loop fusion | flops 3145728 | bytes 8417280 | tf_op jit(solution)/shard_map/jit(_where)/select_n | solution.py:200
  8.8 13.3 %collective-permute-start.2 = (f32[64,512]{1,0:T(8,128)S(1)}, f32[64,512]{1,0:T(8,128)S(1)}, u32[]{:S(2)}, u32[]{:S(2)}) collective-permute-start(f32[64,512]{1,0:T(8,128)S(1)} %collective-permute-done.refs_3_), channel_id=1, source_target_pairs={{0,1},{1,0},{2,3},{3,2},{4,5},{5,4},{6,7},{7,6},{8,9},{9,8},{10,11... | collective-permute-start | bytes 393224 | tf_op jit(solution)/shard_map/ppermute | solution.py:27
  29.9 3.6 %collective-permute-start.4 = (f32[64,512]{1,0:T(8,128)S(1)}, f32[64,512]{1,0:T(8,128)S(1)}, u32[]{:S(2)}, u32[]{:S(2)}) collective-permute-start(f32[64,512]{1,0:T(8,128)S(1)} %collective-permute-done.refs_3_), channel_id=1, source_target_pairs={{0,6},{1,7},{2,4},{3,5},{4,2},{5,3},{6,0},{7,1},{8,14},{9,15},{10,... | collective-permute-start | bytes 393224 | tf_op jit(solution)/shard_map/ppermute | solution.py:27
  35.3 3.2 %collective-permute-done.4.refs_3_ = f32[64,512]{1,0:T(8,128)S(1)} collective-permute-done((f32[64,512]{1,0:T(8,128)S(1)}, f32[64,512]{1,0:T(8,128)S(1)}, u32[]{:S(2)}, u32[]{:S(2)}) %collective-permute-start.4) | collective-permute-done | bytes 131104 | tf_op jit(solution)/shard_map/ppermute | solution.py:27
  38.5 3.2 %collective-permute-done.3.refs_0_ = f32[64,512]{1,0:T(8,128)S(1)} collective-permute-done((f32[64,512]{1,0:T(8,128)S(1)}, f32[64,512]{1,0:T(8,128)S(1)}, u32[]{:S(2)}, u32[]{:S(2)}) %collective-permute-start.3) | collective-permute-done | bytes 131104 | tf_op jit(solution)/shard_map/ppermute | solution.py:27
  41.7 2.6 %collective-permute-start.11 = (f32[16,2048]{1,0:T(8,128)S(1)}, f32[16,2048]{1,0:T(8,128)S(1)}, u32[]{:S(2)}, u32[]{:S(2)}) collective-permute-start(f32[16,2048]{1,0:T(8,128)S(1)} %get-tuple-element.39), channel_id=1, source_target_pairs={{0,32},{1,33},{2,34},{3,35},{4,36},{5,37},{6,38},{7,39},{8,40},{9,... | collective-permute-start | bytes 393224 | tf_op jit(solution)/shard_map/ppermute | solution.py:27
  44.7 2.5 %fusion.14 = f32[320,2048]{1,0:T(8,128)S(1)} fusion(f32[320,512]{1,0:T(8,128)S(1)} %constant_dynamic-update-slice_fusion, f32[512,2048]{1,0:T(8,128)S(1)} %fusion.refs_10_), kind=kOutput, calls=%fused_computation.50 | convolution fusion | flops 2013265920 | bytes 7471104 | tf_op jit(solution)/shard_map/dot_general | solution.py:78
  49.7 3.4 %collective-permute-start.13 = (f32[32,2048]{1,0:T(8,128)S(1)}, f32[32,2048]{1,0:T(8,128)S(1)}, u32[]{:S(2)}, u32[]{:S(2)}) collective-permute-start(f32[32,2048]{1,0:T(8,128)S(1)} %get-tuple-element.43), channel_id=1, source_target_pairs={{0,32},{1,33},{2,34},{3,35},{4,36},{5,37},{6,38},{7,39},{8,40},{9,... | collective-permute-start | bytes 786440 | tf_op jit(solution)/shard_map/ppermute | solution.py:27
  53.1 4.2 %collective-permute-done.13 = f32[32,2048]{1,0:T(8,128)S(1)} collective-permute-done((f32[32,2048]{1,0:T(8,128)S(1)}, f32[32,2048]{1,0:T(8,128)S(1)}, u32[]{:S(2)}, u32[]{:S(2)}) %collective-permute-start.13) | collective-permute-done | bytes 262176 | tf_op jit(solution)/shard_map/ppermute | solution.py:27
  57.4 3.3 %collective-permute-done.14 = f32[32,2048]{1,0:T(8,128)S(1)} collective-permute-done((f32[32,2048]{1,0:T(8,128)S(1)}, f32[32,2048]{1,0:T(8,128)S(1)}, u32[]{:S(2)}, u32[]{:S(2)}) %collective-permute-start.14) | collective-permute-done | bytes 262176 | tf_op jit(solution)/shard_map/ppermute | solution.py:27
  61.0 2.4 %collective-permute-start.15 = (f32[32,2048]{1,0:T(8,128)S(1)}, f32[32,2048]{1,0:T(8,128)S(1)}, u32[]{:S(2)}, u32[]{:S(2)}) collective-permute-start(f32[32,2048]{1,0:T(8,128)S(1)} %get-tuple-element.47), channel_id=1, source_target_pairs={{0,32},{1,33},{2,34},{3,35},{4,36},{5,37},{6,38},{7,39},{8,40},{9,... | collective-permute-start | bytes 786440 | tf_op jit(solution)/shard_map/ppermute | solution.py:27
  63.4 4.1 %collective-permute-done.15 = f32[32,2048]{1,0:T(8,128)S(1)} collective-permute-done((f32[32,2048]{1,0:T(8,128)S(1)}, f32[32,2048]{1,0:T(8,128)S(1)}, u32[]{:S(2)}, u32[]{:S(2)}) %collective-permute-start.15) | collective-permute-done | bytes 262176 | tf_op jit(solution)/shard_map/ppermute | solution.py:27
  67.4 3.9 %collective-permute-done.16 = f32[32,2048]{1,0:T(8,128)S(1)} collective-permute-done((f32[32,2048]{1,0:T(8,128)S(1)}, f32[32,2048]{1,0:T(8,128)S(1)}, u32[]{:S(2)}, u32[]{:S(2)}) %collective-permute-start.16) | collective-permute-done | bytes 262176 | tf_op jit(solution)/shard_map/ppermute | solution.py:27
  73.5 4.3 %collective-permute-done.17 = f32[32,2048]{1,0:T(8,128)S(1)} collective-permute-done((f32[32,2048]{1,0:T(8,128)S(1)}, f32[32,2048]{1,0:T(8,128)S(1)}, u32[]{:S(2)}, u32[]{:S(2)}) %collective-permute-start.17) | collective-permute-done | bytes 262176 | tf_op jit(solution)/shard_map/ppermute | solution.py:27
  79.7 2.9 %collective-permute-start.19 = (f32[32,2048]{1,0:T(8,128)S(1)}, f32[32,2048]{1,0:T(8,128)S(1)}, u32[]{:S(2)}, u32[]{:S(2)}) collective-permute-start(f32[32,2048]{1,0:T(8,128)S(1)} %fusion.8), channel_id=1, source_target_pairs={{0,16},{1,17},{2,18},{3,19},{4,20},{5,21},{6,22},{7,23},{8,24},{9,... | collective-permute-start | bytes 786440 | tf_op jit(solution)/shard_map/ppermute | solution.py:27
  82.6 5.0 %collective-permute-done.19 = f32[32,2048]{1,0:T(8,128)S(1)} collective-permute-done((f32[32,2048]{1,0:T(8,128)S(1)}, f32[32,2048]{1,0:T(8,128)S(1)}, u32[]{:S(2)}, u32[]{:S(2)}) %collective-permute-start.19) | collective-permute-done | bytes 262176 | tf_op jit(solution)/shard_map/ppermute | solution.py:27
  89.8 5.7 %collective-permute-done.26 = f32[32,2048]{1,0:T(8,128)S(1)} collective-permute-done((f32[32,2048]{1,0:T(8,128)S(1)}, f32[32,2048]{1,0:T(8,128)S(1)}, u32[]{:S(2)}, u32[]{:S(2)}) %collective-permute-start.26) | collective-permute-done | bytes 262176 | tf_op jit(solution)/shard_map/ppermute | solution.py:27
  95.5 2.2 %collective-permute-done.27 = f32[32,2048]{1,0:T(8,128)S(1)} collective-permute-done((f32[32,2048]{1,0:T(8,128)S(1)}, f32[32,2048]{1,0:T(8,128)S(1)}, u32[]{:S(2)}, u32[]{:S(2)}) %collective-permute-start.27) | collective-permute-done | bytes 262176 | tf_op jit(solution)/shard_map/ppermute | solution.py:27
  99.7 3.0 %collective-permute-start.20 = (f32[32,1024]{1,0:T(8,128)S(1)}, f32[32,1024]{1,0:T(8,128)S(1)}, u32[]{:S(2)}, u32[]{:S(2)}) collective-permute-start(f32[32,1024]{1,0:T(8,128)S(1)} %constant_dynamic-slice_fusion.1), channel_id=1, source_target_pairs={{0,0},{1,33},{2,66},{3,99},{4,132},{5,165},{6,198},{7,231},{8,8},{... | collective-permute-start | bytes 393224 | tf_op jit(solution)/shard_map/ppermute | solution.py:27
  102.7 5.4 %collective-permute-done.20 = f32[32,1024]{1,0:T(8,128)S(1)} collective-permute-done((f32[32,1024]{1,0:T(8,128)S(1)}, f32[32,1024]{1,0:T(8,128)S(1)}, u32[]{:S(2)}, u32[]{:S(2)}) %collective-permute-start.20) | collective-permute-done | bytes 131104 | tf_op jit(solution)/shard_map/ppermute | solution.py:27
  109.9 4.6 %collective-permute-start.31 = (f32[32,2048]{1,0:T(8,128)S(1)}, f32[32,2048]{1,0:T(8,128)S(1)}, u32[]{:S(2)}, u32[]{:S(2)}) collective-permute-start(f32[32,2048]{1,0:T(8,128)S(1)} %collective-permute-done.29), channel_id=1, source_target_pairs={{0,224},{1,225},{2,226},{3,227},{4,228},{5,229},{6,230},{7,231},{8... | collective-permute-start | bytes 786440 | tf_op jit(solution)/shard_map/ppermute | solution.py:27
  114.7 4.1 %collective-permute-done.30 = f32[32,2048]{1,0:T(8,128)S(1)} collective-permute-done((f32[32,2048]{1,0:T(8,128)S(1)}, f32[32,2048]{1,0:T(8,128)S(1)}, u32[]{:S(2)}, u32[]{:S(2)}) %collective-permute-start.30) | collective-permute-done | bytes 262176 | tf_op jit(solution)/shard_map/ppermute | solution.py:27
  119.4 3.3 %collective-permute-start.33 = (f32[16,2048]{1,0:T(8,128)S(1)}, f32[16,2048]{1,0:T(8,128)S(1)}, u32[]{:S(2)}, u32[]{:S(2)}) collective-permute-start(f32[16,2048]{1,0:T(8,128)S(1)} %slice.51), channel_id=1, source_target_pairs={{0,224},{1,225},{2,226},{3,227},{4,228},{5,229},{6,230},{7,231},{8... | collective-permute-start | bytes 393224 | tf_op jit(solution)/shard_map/ppermute | solution.py:27
  122.7 2.8 %collective-permute-done.32 = f32[16,2048]{1,0:T(8,128)S(1)} collective-permute-done((f32[16,2048]{1,0:T(8,128)S(1)}, f32[16,2048]{1,0:T(8,128)S(1)}, u32[]{:S(2)}, u32[]{:S(2)}) %collective-permute-start.32) | collective-permute-done | bytes 131104 | tf_op jit(solution)/shard_map/ppermute | solution.py:27
  125.7 5.8 %collective-permute-start.22 = (f32[64,512]{1,0:T(8,128)S(1)}, f32[64,512]{1,0:T(8,128)S(1)}, u32[]{:S(2)}, u32[]{:S(2)}) collective-permute-start(f32[64,512]{1,0:T(8,128)S(1)} %bitcast.71), channel_id=1, source_target_pairs={{0,4},{1,5},{2,6},{3,7},{4,0},{5,1},{6,2},{7,3},{8,12},{9,13},{10,... | collective-permute-start | bytes 393224 | tf_op jit(solution)/shard_map/ppermute | solution.py:27
  131.5 4.2 %collective-permute-done.22 = f32[64,512]{1,0:T(8,128)S(1)} collective-permute-done((f32[64,512]{1,0:T(8,128)S(1)}, f32[64,512]{1,0:T(8,128)S(1)}, u32[]{:S(2)}, u32[]{:S(2)}) %collective-permute-start.22) | collective-permute-done | bytes 131104 | tf_op jit(solution)/shard_map/ppermute | solution.py:27
  136.4 4.1 %collective-permute-start.24 = (f32[128,512]{1,0:T(8,128)}, f32[128,512]{1,0:T(8,128)}, u32[]{:S(2)}, u32[]{:S(2)}) collective-permute-start(f32[128,512]{1,0:T(8,128)} %pad_maximum_fusion.1.refs_4_), channel_id=1, source_target_pairs={{0,3},{1,0},{2,1},{3,2},{4,7},{5,4},{6,5},{7,6},{8,11},{9,8},{10,9... | collective-permute-start | bytes 786440 | tf_op jit(solution)/shard_map/ppermute | solution.py:27
  140.9 5.6 %collective-permute-done.24.refs_4_ = f32[128,512]{1,0:T(8,128)} collective-permute-done((f32[128,512]{1,0:T(8,128)}, f32[128,512]{1,0:T(8,128)}, u32[]{:S(2)}, u32[]{:S(2)}) %collective-permute-start.24) | collective-permute-done | bytes 262176 | tf_op jit(solution)/shard_map/ppermute | solution.py:27
  146.5 3.4 %collective-permute-done.23.refs_5_ = f32[128,512]{1,0:T(8,128)} collective-permute-done((f32[128,512]{1,0:T(8,128)}, f32[128,512]{1,0:T(8,128)}, u32[]{:S(2)}, u32[]{:S(2)}) %collective-permute-start.23) | collective-permute-done | bytes 262176 | tf_op jit(solution)/shard_map/ppermute | solution.py:27
  149.9 8.4 %product.2.refs_9_ = f32[512,2048]{1,0:T(8,128)} custom-call(s32[6]{0:T(128)S(1)} %stack.49.at, f32[64,512]{1,0:T(8,128)} %copy-done.5, f32[64,512]{1,0:T(8,128)} %copy-done.7, f32[64,512]{1,0:T(8,128)} %copy-done.6, f32[64,512]{1,0:T(8,128)} %copy-done.8, f32[128,512]{1,0:T(8,128)} %pad_maximum_fusion.1.refs_4_, ...), custom_call_target="tpu_custom_call" | custom-call | flops 3221225472 | bytes 9437184 | tf_op jit(solution)/shard_map/product/pallas_call | solution.py:135
  158.6 10.3 %product.3 = f32[512,2048]{1,0:T(8,128)} custom-call(s32[6]{0:T(128)S(1)} %stack.44.at, f32[64,512]{1,0:T(8,128)} %copy-done.4, f32[64,512]{1,0:T(8,128)} %copy-done.3, f32[64,512]{1,0:T(8,128)} %copy-done.2, f32[64,512]{1,0:T(8,128)} %copy-done.1, f32[128,512]{1,0:T(8,128)} %collective-permute-done.24.refs_4_, ...), custom_call_target="tpu_custom_call" | custom-call | flops 3221225472 | bytes 22020096 | tf_op jit(solution)/shard_map/product/pallas_call | solution.py:135
  (106 shorter events, 27.8 us)
Async XLA Ops:
  0.9 7.9 %collective-permute-start = (f32[64,512]{1,0:T(8,128)S(1)}, f32[64,512]{1,0:T(8,128)S(1)}, u32[]{:S(2)}, u32[]{:S(2)}) collective-permute-start(f32[64,512]{1,0:T(8,128)S(1)} %dynamic_slice.33), channel_id=1, source_target_pairs={{0,0},{1,33},{2,66},{3,99},{4,132},{5,165},{6,198},{7,231},{8,8},{... | collective-permute-start | bytes 393224 | tf_op jit(solution)/shard_map/ppermute | solution.py:27
  8.8 16.6 %collective-permute-start.2 = (f32[64,512]{1,0:T(8,128)S(1)}, f32[64,512]{1,0:T(8,128)S(1)}, u32[]{:S(2)}, u32[]{:S(2)}) collective-permute-start(f32[64,512]{1,0:T(8,128)S(1)} %collective-permute-done.refs_3_), channel_id=1, source_target_pairs={{0,1},{1,0},{2,3},{3,2},{4,5},{5,4},{6,7},{7,6},{8,9},{9,8},{10,11... | collective-permute-start | bytes 393224 | tf_op jit(solution)/shard_map/ppermute | solution.py:27
  23.6 11.5 %collective-permute-start.10 = (f32[1,1,32,2048]{3,2,1,0:T(8,128)S(1)}, f32[1,1,32,2048]{3,2,1,0:T(8,128)S(1)}, u32[]{:S(2)}, u32[]{:S(2)}) collective-permute-start(f32[1,1,32,2048]{3,2,1,0:T(8,128)S(1)} %constant_dynamic-slice_fusion.2), channel_id=1, source_target_pairs={{0,8},{1,9},{2,10},{3,11},{4,12},{5,13},{6,14},{7,15},{8,0},{9,1},... | collective-permute-start | bytes 786440 | tf_op jit(solution)/shard_map/ppermute | solution.py:27
  27.0 17.7 %collective-permute-start.7 = (f32[64,512]{1,0:T(8,128)S(1)}, f32[64,512]{1,0:T(8,128)S(1)}, u32[]{:S(2)}, u32[]{:S(2)}) collective-permute-start(f32[64,512]{1,0:T(8,128)S(1)} %collective-permute-done.refs_3_), channel_id=1, source_target_pairs={{0,4},{1,5},{2,6},{3,7},{4,0},{5,1},{6,2},{7,3},{8,12},{9,13},{10,... | collective-permute-start | bytes 393224 | tf_op jit(solution)/shard_map/ppermute | solution.py:27
  27.0 17.6 %collective-permute-start.6 = (f32[64,512]{1,0:T(8,128)S(1)}, f32[64,512]{1,0:T(8,128)S(1)}, u32[]{:S(2)}, u32[]{:S(2)}) collective-permute-start(f32[64,512]{1,0:T(8,128)S(1)} %collective-permute-done.refs_3_), channel_id=1, source_target_pairs={{0,3},{1,2},{2,1},{3,0},{4,7},{5,6},{6,5},{7,4},{8,11},{9,10},{10,... | collective-permute-start | bytes 393224 | tf_op jit(solution)/shard_map/ppermute | solution.py:27
  28.6 15.7 %collective-permute-start.5 = (f32[64,512]{1,0:T(8,128)S(1)}, f32[64,512]{1,0:T(8,128)S(1)}, u32[]{:S(2)}, u32[]{:S(2)}) collective-permute-start(f32[64,512]{1,0:T(8,128)S(1)} %collective-permute-done.refs_3_), channel_id=1, source_target_pairs={{0,5},{1,4},{2,7},{3,6},{4,1},{5,0},{6,3},{7,2},{8,13},{9,12},{10,... | collective-permute-start | bytes 393224 | tf_op jit(solution)/shard_map/ppermute | solution.py:27
  29.9 8.5 %collective-permute-start.4 = (f32[64,512]{1,0:T(8,128)S(1)}, f32[64,512]{1,0:T(8,128)S(1)}, u32[]{:S(2)}, u32[]{:S(2)}) collective-permute-start(f32[64,512]{1,0:T(8,128)S(1)} %collective-permute-done.refs_3_), channel_id=1, source_target_pairs={{0,6},{1,7},{2,4},{3,5},{4,2},{5,3},{6,0},{7,1},{8,14},{9,15},{10,... | collective-permute-start | bytes 393224 | tf_op jit(solution)/shard_map/ppermute | solution.py:27
  35.1 6.6 %collective-permute-start.3 = (f32[64,512]{1,0:T(8,128)S(1)}, f32[64,512]{1,0:T(8,128)S(1)}, u32[]{:S(2)}, u32[]{:S(2)}) collective-permute-start(f32[64,512]{1,0:T(8,128)S(1)} %collective-permute-done.refs_3_), channel_id=1, source_target_pairs={{0,2},{1,3},{2,0},{3,1},{4,6},{5,7},{6,4},{7,5},{8,10},{9,11},{10,... | collective-permute-start | bytes 393224 | tf_op jit(solution)/shard_map/ppermute | solution.py:27
  38.4 11.1 %collective-permute-start.9 = (f32[2,1,32,2048]{3,2,1,0:T(8,128)S(1)}, f32[2,1,32,2048]{3,2,1,0:T(8,128)S(1)}, u32[]{:S(2)}, u32[]{:S(2)}) collective-permute-start(f32[2,1,32,2048]{3,2,1,0:T(8,128)S(1)} %constant_dynamic-slice_fusion.3), channel_id=1, source_target_pairs={{0,8},{1,9},{2,10},{3,11},{4,12},{5,13},{6,14},{7,15},{8,0},{9,1},... | collective-permute-start | bytes 1572872 | tf_op jit(solution)/shard_map/ppermute | solution.py:27
  47.4 13.3 %collective-permute-start.8 = (f32[5,1,32,2048]{3,2,1,0:T(8,128)S(1)}, f32[5,1,32,2048]{3,2,1,0:T(8,128)S(1)}, u32[]{:S(2)}, u32[]{:S(2)}) collective-permute-start(f32[5,1,32,2048]{3,2,1,0:T(8,128)S(1)} %constant_dynamic-slice_fusion.4), channel_id=1, source_target_pairs={{0,8},{1,9},{2,10},{3,11},{4,12},{5,13},{6,14},{7,15},{8,0},{9,1},... | collective-permute-start | bytes 3932168 | tf_op jit(solution)/shard_map/ppermute | solution.py:27
  49.7 7.7 %collective-permute-start.13 = (f32[32,2048]{1,0:T(8,128)S(1)}, f32[32,2048]{1,0:T(8,128)S(1)}, u32[]{:S(2)}, u32[]{:S(2)}) collective-permute-start(f32[32,2048]{1,0:T(8,128)S(1)} %get-tuple-element.43), channel_id=1, source_target_pairs={{0,32},{1,33},{2,34},{3,35},{4,36},{5,37},{6,38},{7,39},{8,40},{9,... | collective-permute-start | bytes 786440 | tf_op jit(solution)/shard_map/ppermute | solution.py:27
  53.1 7.6 %collective-permute-start.14 = (f32[32,2048]{1,0:T(8,128)S(1)}, f32[32,2048]{1,0:T(8,128)S(1)}, u32[]{:S(2)}, u32[]{:S(2)}) collective-permute-start(f32[32,2048]{1,0:T(8,128)S(1)} %get-tuple-element.44), channel_id=1, source_target_pairs={{0,224},{1,225},{2,226},{3,227},{4,228},{5,229},{6,230},{7,231},{8... | collective-permute-start | bytes 786440 | tf_op jit(solution)/shard_map/ppermute | solution.py:27
  61.0 6.4 %collective-permute-start.15 = (f32[32,2048]{1,0:T(8,128)S(1)}, f32[32,2048]{1,0:T(8,128)S(1)}, u32[]{:S(2)}, u32[]{:S(2)}) collective-permute-start(f32[32,2048]{1,0:T(8,128)S(1)} %get-tuple-element.47), channel_id=1, source_target_pairs={{0,32},{1,33},{2,34},{3,35},{4,36},{5,37},{6,38},{7,39},{8,40},{9,... | collective-permute-start | bytes 786440 | tf_op jit(solution)/shard_map/ppermute | solution.py:27
  63.4 8.0 %collective-permute-start.16 = (f32[32,2048]{1,0:T(8,128)S(1)}, f32[32,2048]{1,0:T(8,128)S(1)}, u32[]{:S(2)}, u32[]{:S(2)}) collective-permute-start(f32[32,2048]{1,0:T(8,128)S(1)} %get-tuple-element.48), channel_id=1, source_target_pairs={{0,224},{1,225},{2,226},{3,227},{4,228},{5,229},{6,230},{7,231},{8... | collective-permute-start | bytes 786440 | tf_op jit(solution)/shard_map/ppermute | solution.py:27
  71.4 6.4 %collective-permute-start.17 = (f32[32,2048]{1,0:T(8,128)S(1)}, f32[32,2048]{1,0:T(8,128)S(1)}, u32[]{:S(2)}, u32[]{:S(2)}) collective-permute-start(f32[32,2048]{1,0:T(8,128)S(1)} %get-tuple-element.51), channel_id=1, source_target_pairs={{0,32},{1,33},{2,34},{3,35},{4,36},{5,37},{6,38},{7,39},{8,40},{9,... | collective-permute-start | bytes 786440 | tf_op jit(solution)/shard_map/ppermute | solution.py:27
  73.3 6.4 %collective-permute-start.18 = (f32[32,2048]{1,0:T(8,128)S(1)}, f32[32,2048]{1,0:T(8,128)S(1)}, u32[]{:S(2)}, u32[]{:S(2)}) collective-permute-start(f32[32,2048]{1,0:T(8,128)S(1)} %get-tuple-element.52), channel_id=1, source_target_pairs={{0,224},{1,225},{2,226},{3,227},{4,228},{5,229},{6,230},{7,231},{8... | collective-permute-start | bytes 786440 | tf_op jit(solution)/shard_map/ppermute | solution.py:27
  79.7 8.0 %collective-permute-start.19 = (f32[32,2048]{1,0:T(8,128)S(1)}, f32[32,2048]{1,0:T(8,128)S(1)}, u32[]{:S(2)}, u32[]{:S(2)}) collective-permute-start(f32[32,2048]{1,0:T(8,128)S(1)} %fusion.8), channel_id=1, source_target_pairs={{0,16},{1,17},{2,18},{3,19},{4,20},{5,21},{6,22},{7,23},{8,24},{9,... | collective-permute-start | bytes 786440 | tf_op jit(solution)/shard_map/ppermute | solution.py:27
  87.7 7.8 %collective-permute-start.26 = (f32[32,2048]{1,0:T(8,128)S(1)}, f32[32,2048]{1,0:T(8,128)S(1)}, u32[]{:S(2)}, u32[]{:S(2)}) collective-permute-start(f32[32,2048]{1,0:T(8,128)S(1)} %add.194), channel_id=1, source_target_pairs={{0,32},{1,33},{2,34},{3,35},{4,36},{5,37},{6,38},{7,39},{8,40},{9,... | collective-permute-start | bytes 786440 | tf_op jit(solution)/shard_map/ppermute | solution.py:27
  89.6 8.1 %collective-permute-start.27 = (f32[32,2048]{1,0:T(8,128)S(1)}, f32[32,2048]{1,0:T(8,128)S(1)}, u32[]{:S(2)}, u32[]{:S(2)}) collective-permute-start(f32[32,2048]{1,0:T(8,128)S(1)} %add.194), channel_id=1, source_target_pairs={{0,224},{1,225},{2,226},{3,227},{4,228},{5,229},{6,230},{7,231},{8... | collective-permute-start | bytes 786440 | tf_op jit(solution)/shard_map/ppermute | solution.py:27
  97.7 10.4 %collective-permute-start.28 = (f32[32,2048]{1,0:T(8,128)S(1)}, f32[32,2048]{1,0:T(8,128)S(1)}, u32[]{:S(2)}, u32[]{:S(2)}) collective-permute-start(f32[32,2048]{1,0:T(8,128)S(1)} %collective-permute-done.26), channel_id=1, source_target_pairs={{0,32},{1,33},{2,34},{3,35},{4,36},{5,37},{6,38},{7,39},{8,40},{9,... | collective-permute-start | bytes 786440 | tf_op jit(solution)/shard_map/ppermute | solution.py:27
  98.9 9.2 %collective-permute-start.29 = (f32[32,2048]{1,0:T(8,128)S(1)}, f32[32,2048]{1,0:T(8,128)S(1)}, u32[]{:S(2)}, u32[]{:S(2)}) collective-permute-start(f32[32,2048]{1,0:T(8,128)S(1)} %collective-permute-done.27), channel_id=1, source_target_pairs={{0,224},{1,225},{2,226},{3,227},{4,228},{5,229},{6,230},{7,231},{8... | collective-permute-start | bytes 786440 | tf_op jit(solution)/shard_map/ppermute | solution.py:27
  99.7 8.4 %collective-permute-start.20 = (f32[32,1024]{1,0:T(8,128)S(1)}, f32[32,1024]{1,0:T(8,128)S(1)}, u32[]{:S(2)}, u32[]{:S(2)}) collective-permute-start(f32[32,1024]{1,0:T(8,128)S(1)} %constant_dynamic-slice_fusion.1), channel_id=1, source_target_pairs={{0,0},{1,33},{2,66},{3,99},{4,132},{5,165},{6,198},{7,231},{8,8},{... | collective-permute-start | bytes 393224 | tf_op jit(solution)/shard_map/ppermute | solution.py:27
  108.1 17.6 %collective-permute-start.21 = (f32[32,512]{1,0:T(8,128)S(1)}, f32[32,512]{1,0:T(8,128)S(1)}, u32[]{:S(2)}, u32[]{:S(2)}) collective-permute-start(f32[32,512]{1,0:T(8,128)S(1)} %constant_dynamic-slice_fusion), channel_id=1, source_target_pairs={{0,8},{1,9},{2,10},{3,11},{4,12},{5,13},{6,14},{7,15},{8,0},{9,1},... | collective-permute-start | bytes 196616 | tf_op jit(solution)/shard_map/ppermute | solution.py:27
  108.1 10.7 %collective-permute-start.30 = (f32[32,2048]{1,0:T(8,128)S(1)}, f32[32,2048]{1,0:T(8,128)S(1)}, u32[]{:S(2)}, u32[]{:S(2)}) collective-permute-start(f32[32,2048]{1,0:T(8,128)S(1)} %collective-permute-done.28), channel_id=1, source_target_pairs={{0,32},{1,33},{2,34},{3,35},{4,36},{5,37},{6,38},{7,39},{8,40},{9,... | collective-permute-start | bytes 786440 | tf_op jit(solution)/shard_map/ppermute | solution.py:27
  109.9 8.9 %collective-permute-start.31 = (f32[32,2048]{1,0:T(8,128)S(1)}, f32[32,2048]{1,0:T(8,128)S(1)}, u32[]{:S(2)}, u32[]{:S(2)}) collective-permute-start(f32[32,2048]{1,0:T(8,128)S(1)} %collective-permute-done.29), channel_id=1, source_target_pairs={{0,224},{1,225},{2,226},{3,227},{4,228},{5,229},{6,230},{7,231},{8... | collective-permute-start | bytes 786440 | tf_op jit(solution)/shard_map/ppermute | solution.py:27
  114.6 35.3 %collective-permute-start.35 = (f32[128,2048]{1,0:T(8,128)S(1)}, f32[128,2048]{1,0:T(8,128)}, u32[]{:S(2)}, u32[]{:S(2)}) collective-permute-start(f32[128,2048]{1,0:T(8,128)S(1)} %pad_maximum_fusion.refs_6_), channel_id=1, source_target_pairs={{0,8},{1,9},{2,10},{3,11},{4,12},{5,13},{6,14},{7,15},{8,0},{9,1},... | collective-permute-start | bytes 3145736 | tf_op jit(solution)/shard_map/ppermute | solution.py:27
  118.9 6.6 %collective-permute-start.32 = (f32[16,2048]{1,0:T(8,128)S(1)}, f32[16,2048]{1,0:T(8,128)S(1)}, u32[]{:S(2)}, u32[]{:S(2)}) collective-permute-start(f32[16,2048]{1,0:T(8,128)S(1)} %slice.50), channel_id=1, source_target_pairs={{0,32},{1,33},{2,34},{3,35},{4,36},{5,37},{6,38},{7,39},{8,40},{9,... | collective-permute-start | bytes 393224 | tf_op jit(solution)/shard_map/ppermute | solution.py:27
  125.5 33.1 %collective-permute-start.34 = (f32[128,2048]{1,0:T(8,128)S(1)}, f32[128,2048]{1,0:T(8,128)S(1)}, u32[]{:S(2)}, u32[]{:S(2)}) collective-permute-start(f32[128,2048]{1,0:T(8,128)S(1)} %constant_dynamic-update-slice_fusion.5.refs_6_), channel_id=1, source_target_pairs={{0,8},{1,9},{2,10},{3,11},{4,12},{5,13},{6,14},{7,15},{8,0},{9,1},... | collective-permute-start | bytes 3145736 | tf_op jit(solution)/shard_map/ppermute | solution.py:27
  125.7 10.0 %collective-permute-start.22 = (f32[64,512]{1,0:T(8,128)S(1)}, f32[64,512]{1,0:T(8,128)S(1)}, u32[]{:S(2)}, u32[]{:S(2)}) collective-permute-start(f32[64,512]{1,0:T(8,128)S(1)} %bitcast.71), channel_id=1, source_target_pairs={{0,4},{1,5},{2,6},{3,7},{4,0},{5,1},{6,2},{7,3},{8,12},{9,13},{10,... | collective-permute-start | bytes 393224 | tf_op jit(solution)/shard_map/ppermute | solution.py:27
  136.4 10.1 %collective-permute-start.24 = (f32[128,512]{1,0:T(8,128)}, f32[128,512]{1,0:T(8,128)}, u32[]{:S(2)}, u32[]{:S(2)}) collective-permute-start(f32[128,512]{1,0:T(8,128)} %pad_maximum_fusion.1.refs_4_), channel_id=1, source_target_pairs={{0,3},{1,0},{2,1},{3,2},{4,7},{5,4},{6,5},{7,6},{8,11},{9,8},{10,9... | collective-permute-start | bytes 786440 | tf_op jit(solution)/shard_map/ppermute | solution.py:27
  140.5 9.4 %collective-permute-start.23 = (f32[128,512]{1,0:T(8,128)}, f32[128,512]{1,0:T(8,128)}, u32[]{:S(2)}, u32[]{:S(2)}) collective-permute-start(f32[128,512]{1,0:T(8,128)} %pad_maximum_fusion.1.refs_4_), channel_id=1, source_target_pairs={{0,1},{1,2},{2,3},{3,0},{4,5},{5,6},{6,7},{7,4},{8,9},{9,10},{10,1... | collective-permute-start | bytes 786440 | tf_op jit(solution)/shard_map/ppermute | solution.py:27
  149.9 8.7 %collective-permute-start.25 = (f32[128,512]{1,0:T(8,128)}, f32[128,512]{1,0:T(8,128)S(1)}, u32[]{:S(2)}, u32[]{:S(2)}) collective-permute-start(f32[128,512]{1,0:T(8,128)} %pad_maximum_fusion.1.refs_4_), channel_id=1, source_target_pairs={{0,2},{1,3},{2,0},{3,1},{4,6},{5,7},{6,4},{7,5},{8,10},{9,11},{10,... | collective-permute-start | bytes 786440 | tf_op jit(solution)/shard_map/ppermute | solution.py:27
  (14 other events, 192.5 us)
where the time goes:
time: 170 us; the launch traced here: 169 us
  waiting for transfers between devices  73.4 us (43%)
  starting transfers between devices  64.1 us (38%)
  Pallas kernels  18.7 us (11%)
  matrix products  5.54 us (3%)
  other arithmetic  4.84 us (3%)
  local copies, waits for them, and re-layouts  1.75 us (1%)
    ppermute x36, waiting for transfers between devices, moved(): lax.ppermute(array, ALL, [(place(*at), place(*target(*at))) for at in eve...  73.4 us
    ppermute x36, starting transfers between devices, moved(): lax.ppermute(array, ALL, [(place(*at), place(*target(*at))) for at in eve...  64.1 us
    pallas_call x2, Pallas kernels, product(): pl.pallas_call(functools.partial(product_kernel, scale, (len(xs), len(oth...  18.7 us
    dot_general x3, matrix products, dot(): jnp.dot(left, right, precision=lax.Precision.HIGH, preferred_element_type...  5.54 us
  transfers between devices with their start and end apart: 36, of which 22 were waited for; matrix products, arithmetic and copies ran while one was open for 6% of the time, Pallas kernels for 5%

commit v1 on v0

--- a/solution.py
+++ b/solution.py
@@ -80,33 +80,34 @@
     )
 
 
-def product_kernel(scale, sizes, at, *refs):
-    xs, refs = refs[: sizes[0]], refs[sizes[0] :]
-    others, refs = refs[: sizes[1]], refs[sizes[1] :]
-    ys, samples, refs = refs[:2], refs[2], refs[3:]
-    *final, out, high, low = refs
+def columns_kernel(count, core, *refs):
+    xs, rights, (out, high, low) = refs[:count], refs[count:-3], refs[-3:]
+
+    @pl.when(pl.program_id(0) == 0)
+    def _():
+        half = xs[0].shape[0] // 2
+        rows = []
+        for some in (xs[: count // 2], xs[count // 2 :]):
+            for which in (core[0], 1 - core[0]):
+                rows += [x[pl.ds(pl.multiple_of(which * half, half), half), :] for x in some]
+        high[...], low[...] = split_in_two(jnp.concatenate(rows).T)
+
+    right = jnp.concatenate([part[...] for part in rights])
+    out[...] = in_three((high[...], low[...]), split_in_two(right))
+
+
+def update_kernel(scale, sizes, at, *refs):
+    lefts, refs = refs[: sizes[0]], refs[sizes[0] :]
+    rights, refs = refs[: sizes[1]], refs[sizes[1] :]
+    addend, omega, diag, out, high, low = refs
     step = pl.program_id(0)
-    piece_rows = xs[0].shape[0]
-    half = piece_rows // 2
 
     @pl.when(step == 0)
     def _():
-        rows = []
-        for which in (at[1], 1 - at[1]):
-            rows += [x[pl.ds(pl.multiple_of(which * half, half), half), :] for x in xs]
-        rows += [other[...] for other in others]
-        high[...], low[...] = split_in_two(jnp.concatenate(rows).T)
-
-    right = [y[...] for y in ys]
-    for i in range(high.shape[1] // piece_rows - len(xs)):
-        first = pl.multiple_of(at[2 + i] * piece_rows, piece_rows)
-        right.append(samples[pl.ds(first, piece_rows), :])
-    made = in_three((high[...], low[...]), split_in_two(jnp.concatenate(right)))
-    if scale is None:
-        out[...] = made
-        return
-    addend, omega, diag = final
-    made = made + addend[...]
+        high[...], low[...] = split_in_two(jnp.concatenate([part[...] for part in lefts]).T)
+
+    right = jnp.concatenate([part[...] for part in rights])
+    made = in_three((high[...], low[...]), split_in_two(right)) + addend[...]
     behind = at[0] - step * LANES
     rows = lax.broadcasted_iota(jnp.int32, made.shape, 0)
     cols = lax.broadcasted_iota(jnp.int32, made.shape, 1)
@@ -117,23 +118,17 @@
     out[...] = jnp.where(on_diag, stepped, stepped - jnp.clip(stepped, -limit, limit))
 
 
-def product(at, xs, others, ys, samples, scale=None, final=()):
-    depth = sum(part.shape[0] for part in (*xs, *others))
-    rows, cols = xs[0].shape[1], samples.shape[1]
-
-    def whole(array):
-        return pl.BlockSpec(array.shape, lambda j, *_: (0, 0))
-
-    def tile(array):
-        return pl.BlockSpec((array.shape[0], LANES), lambda j, *_: (0, j))
-
-    xs, samples = [in_hbm(x) for x in xs], in_hbm(samples)
-    if final:
-        final = [in_hbm(final[0]), in_hbm(final[1]), final[2]]
-    specs = [whole(part) for part in (*xs, *others)] + [tile(part) for part in (*ys, samples)]
-    specs += [whole(part) if part.shape[1] == 1 else tile(part) for part in final]
+def whole(array):
+    return pl.BlockSpec(array.shape, lambda j, *_: (0, 0))
+
+
+def tile(array):
+    return pl.BlockSpec((array.shape[0], LANES), lambda j, *_: (0, j))
+
+
+def call(kernel, scalars, operands, specs, depth, rows, cols, out_shape):
     return pl.pallas_call(
-        functools.partial(product_kernel, scale, (len(xs), len(others))),
+        kernel,
         grid_spec=pltpu.PrefetchScalarGridSpec(
             num_scalar_prefetch=1,
             grid=(cols // LANES,),
@@ -141,15 +136,54 @@
             out_specs=pl.BlockSpec((rows, LANES), lambda j, *_: (0, j)),
             scratch_shapes=[pltpu.VMEM((rows, depth), jnp.bfloat16)] * 2,
         ),
-        out_shape=pltpu.HBM((rows, cols), jnp.float32),
+        out_shape=out_shape,
         cost_estimate=pl.CostEstimate(
             flops=6 * depth * rows * cols,
-            bytes_accessed=4 * (depth * rows + depth * cols + (1 + len(final)) * rows * cols),
+            bytes_accessed=4 * (depth * rows + depth * cols + 2 * rows * cols),
             transcendentals=0,
         ),
         compiler_params=pltpu.CompilerParams(vmem_limit_bytes=16 << 20),
-        name="product",
-    )(at, *xs, *others, *ys, samples, *final)
+    )(scalars, *operands)
+
+
+def columns_product(core, xs, rights):
+    depth = sum(part.shape[0] for part in rights)
+    rows, cols = xs[0].shape[1], rights[0].shape[1]
+    xs = [in_hbm(x) for x in xs]
+    return call(
+        functools.partial(columns_kernel, len(xs)),
+        core.reshape(1),
+        [*xs, *rights],
+        [whole(x) for x in xs] + [tile(part) for part in rights],
+        depth,
+        rows,
+        cols,
+        pltpu.HBM((rows, cols), jnp.float32),
+    )
+
+
+def updated(scale, offset, lefts, samples, order, addend, omega, diag):
+    depth, cols = samples.shape
+    rows = lefts[0].shape[1]
+    samples, addend, omega = in_hbm(samples), in_hbm(addend), in_hbm(omega)
+    piece_rows = depth // len(order)
+
+    def piece(i):
+        return pl.BlockSpec((piece_rows, LANES), lambda j, at: (at[1 + i], j))
+
+    count = len(order)
+    return call(
+        functools.partial(update_kernel, scale, (len(lefts), count)),
+        jnp.stack([offset, *order]),
+        [*lefts, *[samples] * count, addend, omega, diag],
+        [whole(part) for part in lefts]
+        + [piece(i) for i in range(count)]
+        + [tile(addend), tile(omega), whole(diag)],
+        depth,
+        rows,
+        cols,
+        jax.ShapeDtypeStruct((rows, cols), jnp.float32),
+    )
 
 
 NEXT = (3, -3)
@@ -246,31 +280,27 @@
     whole[-3], whole[3] = together(up(whole[-2]), down(whole[2]))
     before, after = along_x(pair, 1), along_x(pair, -1)
     other_near_y = other_core(near_y)
-    offset = row_index * tile_rows - col * tile_cols
+    opposite = along_x(pair, 2)
+    rising, falling = together(up(whole[-3][:cut]), down(whole[3][cut:]))
+    far_y = jnp.concatenate([whole[d] for d in FAR[:-1]] + [rising, falling])
+    other_far_y = other_core(far_y)
+    products = columns_product(
+        core, [pieces[d] for d in NEAR + FAR], [near_y, other_near_y, far_y, other_far_y]
+    )
+
     x_at, side = col % 4, col // 4
     match = [
         flip * 4 + (x_at + by) % 4 for by in (0, -1, 1, 2) for flip in (side, 1 - side)
     ]
-    rising, falling = up(whole[-3][:cut]), down(whole[3][cut:])
-    before, after, pair = together(before, after, pair)
-    opposite = along_x(pair, 2)
-    products = product(
-        jnp.stack([offset, core, *match[:4]]),
-        [pieces[d] for d in NEAR],
-        [pair, before],
-        [near_y, other_near_y],
+    return updated(
+        0.5 / sample_count,
+        row_index * tile_rows - col * tile_cols,
+        [pair, before, after, opposite],
         samples,
-    )
-    far_y = jnp.concatenate([whole[d] for d in FAR[:-1]] + [rising, falling])
-    other_far_y = other_core(far_y)
-    return product(
-        jnp.stack([offset, core, *match[4:]]),
-        [pieces[d] for d in FAR],
-        [after, opposite],
-        [far_y, other_far_y],
-        samples,
-        0.5 / sample_count,
-        [products, omega, diag_entries[:, None]],
+        match,
+        products,
+        omega,
+        diag_entries[:, None],
     )
 
 

time: 170 us -> 177 us (1.041)
  waiting for transfers between devices: 73.4 us -> 81.4 us
    ppermute x36, waiting for transfers between devices: 73.4 us -> 81.4 us  [moved(): lax.ppermute(array, ALL, [(place(*at), place(*target(*at))) for at in eve...]
  transfers between devices with their start and end apart: 36 -> 36, of which waited for: 22 -> 27; matrix products, arithmetic and copies ran while one was open for 6% -> 6% of each run, Pallas kernels for 5% -> 4%
where the time goes in v1:
time: 177 us; the launch traced here: 175 us
  waiting for transfers between devices  81.4 us (46%)
  starting transfers between devices  63.8 us (36%)
  Pallas kernels  17.4 us (10%)
  matrix products  5.52 us (3%)
  other arithmetic  5.02 us (3%)
    ppermute x36, waiting for transfers between devices, moved(): lax.ppermute(array, ALL, [(place(*at), place(*target(*at))) for at in eve...  81.4 us
    ppermute x36, starting transfers between devices, moved(): lax.ppermute(array, ALL, [(place(*at), place(*target(*at))) for at in eve...  63.8 us
    pallas_call x2, Pallas kernels, call(): pl.pallas_call(kernel, grid_spec=pltpu.PrefetchScalarGridSpec(num_scalar_...  17.4 us
    dot_general x3, matrix products, dot(): jnp.dot(left, right, precision=lax.Precision.HIGH, preferred_element_type...  5.52 us
  transfers between devices with their start and end apart: 36, of which 27 were waited for; matrix products, arithmetic and copies ran while one was open for 6% of the time, Pallas kernels for 4%

profile of v1, /device:TPU:32, one launch (start us, length us, event | category | flops | bytes accessed | tf_op | source)
XLA Modules:
  0.0 175.3 jit_solution(14982585044575316902)
XLA Ops:
  0.9 2.9 %collective-permute-start = (f32[64,512]{1,0:T(8,128)S(1)}, f32[64,512]{1,0:T(8,128)S(1)}, u32[]{:S(2)}, u32[]{:S(2)}) collective-permute-start(f32[64,512]{1,0:T(8,128)S(1)} %dynamic_slice.33), channel_id=1, source_target_pairs={{0,0},{1,33},{2,66},{3,99},{4,132},{5,165},{6,198},{7,231},{8,8},{... | collective-permute-start | bytes 393224 | tf_op jit(solution)/shard_map/ppermute | solution.py:27
  4.8 2.7 %fusion.refs_13_ = f32[512,2048]{1,0:T(8,128)S(1)} fusion(f32[512,2048]{1,0:T(8,128)} %param.5, f32[2,2048]{1,0:T(2,128)S(1)} %bitcast.73, f32[512]{0:T(512)} %param.6, s32[2048]{0:T(1024)S(1)} %iota_add_fusion, s32[512]{0:T(512)S(1)} %iota_add_fusion.1), kind=kLoop, calls=%fused_computation.1 | loop fusion | flops 3145728 | bytes 8417280 | tf_op jit(solution)/shard_map/jit(_where)/select_n | solution.py:234
  9.5 12.6 %collective-permute-start.2 = (f32[64,512]{1,0:T(8,128)S(1)}, f32[64,512]{1,0:T(8,128)S(1)}, u32[]{:S(2)}, u32[]{:S(2)}) collective-permute-start(f32[64,512]{1,0:T(8,128)S(1)} %collective-permute-done.refs_7_), channel_id=1, source_target_pairs={{0,1},{1,0},{2,3},{3,2},{4,5},{5,4},{6,7},{7,6},{8,9},{9,8},{10,11... | collective-permute-start | bytes 393224 | tf_op jit(solution)/shard_map/ppermute | solution.py:27
  25.5 2.4 %collective-permute-start.3 = (f32[64,512]{1,0:T(8,128)S(1)}, f32[64,512]{1,0:T(8,128)S(1)}, u32[]{:S(2)}, u32[]{:S(2)}) collective-permute-start(f32[64,512]{1,0:T(8,128)S(1)} %collective-permute-done.refs_7_), channel_id=1, source_target_pairs={{0,6},{1,7},{2,4},{3,5},{4,2},{5,3},{6,0},{7,1},{8,14},{9,15},{10,... | collective-permute-start | bytes 393224 | tf_op jit(solution)/shard_map/ppermute | solution.py:27
  28.6 4.3 %collective-permute-start.5 = (f32[64,512]{1,0:T(8,128)S(1)}, f32[64,512]{1,0:T(8,128)S(1)}, u32[]{:S(2)}, u32[]{:S(2)}) collective-permute-start(f32[64,512]{1,0:T(8,128)S(1)} %collective-permute-done.refs_7_), channel_id=1, source_target_pairs={{0,5},{1,4},{2,7},{3,6},{4,1},{5,0},{6,3},{7,2},{8,13},{9,12},{10,... | collective-permute-start | bytes 393224 | tf_op jit(solution)/shard_map/ppermute | solution.py:27
  36.4 3.2 %collective-permute-done.5.refs_1_ = f32[64,512]{1,0:T(8,128)S(1)} collective-permute-done((f32[64,512]{1,0:T(8,128)S(1)}, f32[64,512]{1,0:T(8,128)S(1)}, u32[]{:S(2)}, u32[]{:S(2)}) %collective-permute-start.5) | collective-permute-done | bytes 131104 | tf_op jit(solution)/shard_map/ppermute | solution.py:27
  40.0 2.7 %collective-permute-done.7.refs_0_ = f32[64,512]{1,0:T(8,128)S(1)} collective-permute-done((f32[64,512]{1,0:T(8,128)S(1)}, f32[64,512]{1,0:T(8,128)S(1)}, u32[]{:S(2)}, u32[]{:S(2)}) %collective-permute-start.7) | collective-permute-done | bytes 131104 | tf_op jit(solution)/shard_map/ppermute | solution.py:27
  42.7 2.5 %fusion.14 = f32[320,2048]{1,0:T(8,128)S(1)} fusion(f32[320,512]{1,0:T(8,128)S(1)} %constant_dynamic-update-slice_fusion, f32[512,2048]{1,0:T(8,128)S(1)} %fusion.refs_13_), kind=kOutput, calls=%fused_computation.50 | convolution fusion | flops 2013265920 | bytes 7471104 | tf_op jit(solution)/shard_map/dot_general | solution.py:78
  45.3 3.0 %collective-permute-start.11 = (f32[16,2048]{1,0:T(8,128)S(1)}, f32[16,2048]{1,0:T(8,128)S(1)}, u32[]{:S(2)}, u32[]{:S(2)}) collective-permute-start(f32[16,2048]{1,0:T(8,128)S(1)} %get-tuple-element.38), channel_id=1, source_target_pairs={{0,32},{1,33},{2,34},{3,35},{4,36},{5,37},{6,38},{7,39},{8,40},{9,... | collective-permute-start | bytes 393224 | tf_op jit(solution)/shard_map/ppermute | solution.py:27
  48.5 2.7 %collective-permute-done.11 = f32[16,2048]{1,0:T(8,128)S(1)} collective-permute-done((f32[16,2048]{1,0:T(8,128)S(1)}, f32[16,2048]{1,0:T(8,128)S(1)}, u32[]{:S(2)}, u32[]{:S(2)}) %collective-permute-start.11) | collective-permute-done | bytes 131104 | tf_op jit(solution)/shard_map/ppermute | solution.py:27
  51.2 2.2 %collective-permute-done.12 = f32[16,2048]{1,0:T(8,128)S(1)} collective-permute-done((f32[16,2048]{1,0:T(8,128)S(1)}, f32[16,2048]{1,0:T(8,128)S(1)}, u32[]{:S(2)}, u32[]{:S(2)}) %collective-permute-start.12) | collective-permute-done | bytes 131104 | tf_op jit(solution)/shard_map/ppermute | solution.py:27
  55.7 5.1 %collective-permute-done.13 = f32[32,2048]{1,0:T(8,128)S(1)} collective-permute-done((f32[32,2048]{1,0:T(8,128)S(1)}, f32[32,2048]{1,0:T(8,128)S(1)}, u32[]{:S(2)}, u32[]{:S(2)}) %collective-permute-start.13) | collective-permute-done | bytes 262176 | tf_op jit(solution)/shard_map/ppermute | solution.py:27
  60.7 3.2 %collective-permute-done.14 = f32[32,2048]{1,0:T(8,128)S(1)} collective-permute-done((f32[32,2048]{1,0:T(8,128)S(1)}, f32[32,2048]{1,0:T(8,128)S(1)}, u32[]{:S(2)}, u32[]{:S(2)}) %collective-permute-start.14) | collective-permute-done | bytes 262176 | tf_op jit(solution)/shard_map/ppermute | solution.py:27
  66.3 4.5 %collective-permute-done.15 = f32[32,2048]{1,0:T(8,128)S(1)} collective-permute-done((f32[32,2048]{1,0:T(8,128)S(1)}, f32[32,2048]{1,0:T(8,128)S(1)}, u32[]{:S(2)}, u32[]{:S(2)}) %collective-permute-start.15) | collective-permute-done | bytes 262176 | tf_op jit(solution)/shard_map/ppermute | solution.py:27
  70.8 2.3 %collective-permute-done.16 = f32[32,2048]{1,0:T(8,128)S(1)} collective-permute-done((f32[32,2048]{1,0:T(8,128)S(1)}, f32[32,2048]{1,0:T(8,128)S(1)}, u32[]{:S(2)}, u32[]{:S(2)}) %collective-permute-start.16) | collective-permute-done | bytes 262176 | tf_op jit(solution)/shard_map/ppermute | solution.py:27
  73.1 2.1 %collective-permute-start.17 = (f32[32,2048]{1,0:T(8,128)S(1)}, f32[32,2048]{1,0:T(8,128)S(1)}, u32[]{:S(2)}, u32[]{:S(2)}) collective-permute-start(f32[32,2048]{1,0:T(8,128)S(1)} %get-tuple-element.50), channel_id=1, source_target_pairs={{0,32},{1,33},{2,34},{3,35},{4,36},{5,37},{6,38},{7,39},{8,40},{9,... | collective-permute-start | bytes 786440 | tf_op jit(solution)/shard_map/ppermute | solution.py:27
  75.2 4.3 %collective-permute-done.17 = f32[32,2048]{1,0:T(8,128)S(1)} collective-permute-done((f32[32,2048]{1,0:T(8,128)S(1)}, f32[32,2048]{1,0:T(8,128)S(1)}, u32[]{:S(2)}, u32[]{:S(2)}) %collective-permute-start.17) | collective-permute-done | bytes 262176 | tf_op jit(solution)/shard_map/ppermute | solution.py:27
  79.5 2.0 %collective-permute-done.18 = f32[32,2048]{1,0:T(8,128)S(1)} collective-permute-done((f32[32,2048]{1,0:T(8,128)S(1)}, f32[32,2048]{1,0:T(8,128)S(1)}, u32[]{:S(2)}, u32[]{:S(2)}) %collective-permute-start.18) | collective-permute-done | bytes 262176 | tf_op jit(solution)/shard_map/ppermute | solution.py:27
  81.6 3.2 %collective-permute-start.19 = (f32[32,2048]{1,0:T(8,128)S(1)}, f32[32,2048]{1,0:T(8,128)S(1)}, u32[]{:S(2)}, u32[]{:S(2)}) collective-permute-start(f32[32,2048]{1,0:T(8,128)S(1)} %fusion.8), channel_id=1, source_target_pairs={{0,16},{1,17},{2,18},{3,19},{4,20},{5,21},{6,22},{7,23},{8,24},{9,... | collective-permute-start | bytes 786440 | tf_op jit(solution)/shard_map/ppermute | solution.py:27
  84.8 4.8 %collective-permute-done.19 = f32[32,2048]{1,0:T(8,128)S(1)} collective-permute-done((f32[32,2048]{1,0:T(8,128)S(1)}, f32[32,2048]{1,0:T(8,128)S(1)}, u32[]{:S(2)}, u32[]{:S(2)}) %collective-permute-start.19) | collective-permute-done | bytes 262176 | tf_op jit(solution)/shard_map/ppermute | solution.py:27
  91.7 6.6 %collective-permute-done.26 = f32[32,2048]{1,0:T(8,128)S(1)} collective-permute-done((f32[32,2048]{1,0:T(8,128)S(1)}, f32[32,2048]{1,0:T(8,128)S(1)}, u32[]{:S(2)}, u32[]{:S(2)}) %collective-permute-start.26) | collective-permute-done | bytes 262176 | tf_op jit(solution)/shard_map/ppermute | solution.py:27
  101.7 5.6 %collective-permute-done.28 = f32[32,2048]{1,0:T(8,128)S(1)} collective-permute-done((f32[32,2048]{1,0:T(8,128)S(1)}, f32[32,2048]{1,0:T(8,128)S(1)}, u32[]{:S(2)}, u32[]{:S(2)}) %collective-permute-start.28) | collective-permute-done | bytes 262176 | tf_op jit(solution)/shard_map/ppermute | solution.py:27
  111.1 4.4 %collective-permute-done.31 = f32[32,2048]{1,0:T(8,128)S(1)} collective-permute-done((f32[32,2048]{1,0:T(8,128)S(1)}, f32[32,2048]{1,0:T(8,128)S(1)}, u32[]{:S(2)}, u32[]{:S(2)}) %collective-permute-start.31) | collective-permute-done | bytes 262176 | tf_op jit(solution)/shard_map/ppermute | solution.py:27
  115.5 2.4 %collective-permute-done.32 = f32[32,2048]{1,0:T(8,128)S(1)} collective-permute-done((f32[32,2048]{1,0:T(8,128)S(1)}, f32[32,2048]{1,0:T(8,128)S(1)}, u32[]{:S(2)}, u32[]{:S(2)}) %collective-permute-start.32) | collective-permute-done | bytes 262176 | tf_op jit(solution)/shard_map/ppermute | solution.py:27
  120.3 2.8 %collective-permute-done.33 = f32[16,2048]{1,0:T(8,128)S(1)} collective-permute-done((f32[16,2048]{1,0:T(8,128)S(1)}, f32[16,2048]{1,0:T(8,128)S(1)}, u32[]{:S(2)}, u32[]{:S(2)}) %collective-permute-start.33) | collective-permute-done | bytes 131104 | tf_op jit(solution)/shard_map/ppermute | solution.py:27
  126.8 5.9 %collective-permute-done.20 = f32[32,1024]{1,0:T(8,128)S(1)} collective-permute-done((f32[32,1024]{1,0:T(8,128)S(1)}, f32[32,1024]{1,0:T(8,128)S(1)}, u32[]{:S(2)}, u32[]{:S(2)}) %collective-permute-start.20) | collective-permute-done | bytes 131104 | tf_op jit(solution)/shard_map/ppermute | solution.py:27
  134.0 8.4 %collective-permute-start.22 = (f32[64,512]{1,0:T(8,128)S(1)}, f32[64,512]{1,0:T(8,128)}, u32[]{:S(2)}, u32[]{:S(2)}) collective-permute-start(f32[64,512]{1,0:T(8,128)S(1)} %bitcast.71), channel_id=1, source_target_pairs={{0,4},{1,5},{2,6},{3,7},{4,0},{5,1},{6,2},{7,3},{8,12},{9,13},{10,... | collective-permute-start | bytes 393224 | tf_op jit(solution)/shard_map/ppermute | solution.py:27
  142.6 3.7 %collective-permute-done.22 = f32[64,512]{1,0:T(8,128)} collective-permute-done((f32[64,512]{1,0:T(8,128)S(1)}, f32[64,512]{1,0:T(8,128)}, u32[]{:S(2)}, u32[]{:S(2)}) %collective-permute-start.22) | collective-permute-done | bytes 131104 | tf_op jit(solution)/shard_map/ppermute | solution.py:27
  147.3 5.2 %collective-permute-start.24 = (f32[128,512]{1,0:T(8,128)S(1)}, f32[128,512]{1,0:T(8,128)S(1)}, u32[]{:S(2)}, u32[]{:S(2)}) collective-permute-start(f32[128,512]{1,0:T(8,128)S(1)} %pad_maximum_fusion.1.refs_0_), channel_id=1, source_target_pairs={{0,3},{1,0},{2,1},{3,2},{4,7},{5,4},{6,5},{7,6},{8,11},{9,8},{10,9... | collective-permute-start | bytes 786440 | tf_op jit(solution)/shard_map/ppermute | solution.py:27
  153.9 7.1 %shard_map.46.refs_12_ = f32[512,2048]{1,0:T(8,128)} custom-call(s32[1]{0:T(128)} %bitcast.25.core, f32[64,512]{1,0:T(8,128)} %copy-done.8, f32[64,512]{1,0:T(8,128)} %copy-done.6, f32[64,512]{1,0:T(8,128)} %copy-done.7, f32[64,512]{1,0:T(8,128)} %copy-done.4, f32[64,512]{1,0:T(8,128)} %copy-done.5, f32[64,512]{1,0:T(8,128)} %copy-done.2, ...), custom_call_target="tpu_custom_call" | custom-call | flops 3221225472 | bytes 13631488 | tf_op jit(solution)/shard_map/pallas_call | solution.py:130
  161.0 2.1 %collective-permute-done.24.refs_2_ = f32[128,512]{1,0:T(8,128)S(1)} collective-permute-done((f32[128,512]{1,0:T(8,128)S(1)}, f32[128,512]{1,0:T(8,128)S(1)}, u32[]{:S(2)}, u32[]{:S(2)}) %collective-permute-start.24) | collective-permute-done | bytes 262176 | tf_op jit(solution)/shard_map/ppermute | solution.py:27
  165.0 10.3 %shard_map.47 = f32[512,2048]{1,0:T(8,128)} custom-call(s32[9]{0:T(128)S(1)} %stack.39.at, f32[128,512]{1,0:T(8,128)S(1)} %pad_maximum_fusion.1.refs_0_, f32[128,512]{1,0:T(8,128)S(1)} %collective-permute-done.23.refs_1_, f32[128,512]{1,0:T(8,128)S(1)} %collective-permute-done.24.refs_2_, f32[128,512]{1,0:T(8,128)S(1)} %collective-permute-done.25.refs_3_, ...), custom_call_target="tpu_custom_call" | custom-call | flops 3221225472 | bytes 13631488 | tf_op jit(solution)/shard_map/pallas_call | solution.py:130
  (105 shorter events, 37.5 us)
Async XLA Ops:
  0.9 7.9 %collective-permute-start = (f32[64,512]{1,0:T(8,128)S(1)}, f32[64,512]{1,0:T(8,128)S(1)}, u32[]{:S(2)}, u32[]{:S(2)}) collective-permute-start(f32[64,512]{1,0:T(8,128)S(1)} %dynamic_slice.33), channel_id=1, source_target_pairs={{0,0},{1,33},{2,66},{3,99},{4,132},{5,165},{6,198},{7,231},{8,8},{... | collective-permute-start | bytes 393224 | tf_op jit(solution)/shard_map/ppermute | solution.py:27
  8.8 15.0 %collective-permute-start.1 = (f32[64,512]{1,0:T(8,128)S(1)}, f32[64,512]{1,0:T(8,128)S(1)}, u32[]{:S(2)}, u32[]{:S(2)}) collective-permute-start(f32[64,512]{1,0:T(8,128)S(1)} %collective-permute-done.refs_7_), channel_id=1, source_target_pairs={{0,7},{1,6},{2,5},{3,4},{4,3},{5,2},{6,1},{7,0},{8,15},{9,14},{10,... | collective-permute-start | bytes 393224 | tf_op jit(solution)/shard_map/ppermute | solution.py:27
  9.5 16.0 %collective-permute-start.2 = (f32[64,512]{1,0:T(8,128)S(1)}, f32[64,512]{1,0:T(8,128)S(1)}, u32[]{:S(2)}, u32[]{:S(2)}) collective-permute-start(f32[64,512]{1,0:T(8,128)S(1)} %collective-permute-done.refs_7_), channel_id=1, source_target_pairs={{0,1},{1,0},{2,3},{3,2},{4,5},{5,4},{6,7},{7,6},{8,9},{9,8},{10,11... | collective-permute-start | bytes 393224 | tf_op jit(solution)/shard_map/ppermute | solution.py:27
  23.7 10.8 %collective-permute-start.10 = (f32[1,1,32,2048]{3,2,1,0:T(8,128)S(1)}, f32[1,1,32,2048]{3,2,1,0:T(8,128)S(1)}, u32[]{:S(2)}, u32[]{:S(2)}) collective-permute-start(f32[1,1,32,2048]{3,2,1,0:T(8,128)S(1)} %constant_dynamic-slice_fusion.2), channel_id=1, source_target_pairs={{0,8},{1,9},{2,10},{3,11},{4,12},{5,13},{6,14},{7,15},{8,0},{9,1},... | collective-permute-start | bytes 786440 | tf_op jit(solution)/shard_map/ppermute | solution.py:27
  25.5 10.7 %collective-permute-start.3 = (f32[64,512]{1,0:T(8,128)S(1)}, f32[64,512]{1,0:T(8,128)S(1)}, u32[]{:S(2)}, u32[]{:S(2)}) collective-permute-start(f32[64,512]{1,0:T(8,128)S(1)} %collective-permute-done.refs_7_), channel_id=1, source_target_pairs={{0,6},{1,7},{2,4},{3,5},{4,2},{5,3},{6,0},{7,1},{8,14},{9,15},{10,... | collective-permute-start | bytes 393224 | tf_op jit(solution)/shard_map/ppermute | solution.py:27
  27.9 8.4 %collective-permute-start.4 = (f32[64,512]{1,0:T(8,128)S(1)}, f32[64,512]{1,0:T(8,128)S(1)}, u32[]{:S(2)}, u32[]{:S(2)}) collective-permute-start(f32[64,512]{1,0:T(8,128)S(1)} %collective-permute-done.refs_7_), channel_id=1, source_target_pairs={{0,2},{1,3},{2,0},{3,1},{4,6},{5,7},{6,4},{7,5},{8,10},{9,11},{10,... | collective-permute-start | bytes 393224 | tf_op jit(solution)/shard_map/ppermute | solution.py:27
  28.6 11.0 %collective-permute-start.5 = (f32[64,512]{1,0:T(8,128)S(1)}, f32[64,512]{1,0:T(8,128)S(1)}, u32[]{:S(2)}, u32[]{:S(2)}) collective-permute-start(f32[64,512]{1,0:T(8,128)S(1)} %collective-permute-done.refs_7_), channel_id=1, source_target_pairs={{0,5},{1,4},{2,7},{3,6},{4,1},{5,0},{6,3},{7,2},{8,13},{9,12},{10,... | collective-permute-start | bytes 393224 | tf_op jit(solution)/shard_map/ppermute | solution.py:27
  32.9 7.1 %collective-permute-start.6 = (f32[64,512]{1,0:T(8,128)S(1)}, f32[64,512]{1,0:T(8,128)S(1)}, u32[]{:S(2)}, u32[]{:S(2)}) collective-permute-start(f32[64,512]{1,0:T(8,128)S(1)} %collective-permute-done.refs_7_), channel_id=1, source_target_pairs={{0,3},{1,2},{2,1},{3,0},{4,7},{5,6},{6,5},{7,4},{8,11},{9,10},{10,... | collective-permute-start | bytes 393224 | tf_op jit(solution)/shard_map/ppermute | solution.py:27
  34.5 8.2 %collective-permute-start.7 = (f32[64,512]{1,0:T(8,128)S(1)}, f32[64,512]{1,0:T(8,128)S(1)}, u32[]{:S(2)}, u32[]{:S(2)}) collective-permute-start(f32[64,512]{1,0:T(8,128)S(1)} %collective-permute-done.refs_7_), channel_id=1, source_target_pairs={{0,4},{1,5},{2,6},{3,7},{4,0},{5,1},{6,2},{7,3},{8,12},{9,13},{10,... | collective-permute-start | bytes 393224 | tf_op jit(solution)/shard_map/ppermute | solution.py:27
  36.2 17.2 %collective-permute-start.9 = (f32[2,1,32,2048]{3,2,1,0:T(8,128)S(1)}, f32[2,1,32,2048]{3,2,1,0:T(8,128)S(1)}, u32[]{:S(2)}, u32[]{:S(2)}) collective-permute-start(f32[2,1,32,2048]{3,2,1,0:T(8,128)S(1)} %constant_dynamic-slice_fusion.3), channel_id=1, source_target_pairs={{0,8},{1,9},{2,10},{3,11},{4,12},{5,13},{6,14},{7,15},{8,0},{9,1},... | collective-permute-start | bytes 1572872 | tf_op jit(solution)/shard_map/ppermute | solution.py:27
  45.3 5.9 %collective-permute-start.11 = (f32[16,2048]{1,0:T(8,128)S(1)}, f32[16,2048]{1,0:T(8,128)S(1)}, u32[]{:S(2)}, u32[]{:S(2)}) collective-permute-start(f32[16,2048]{1,0:T(8,128)S(1)} %get-tuple-element.38), channel_id=1, source_target_pairs={{0,32},{1,33},{2,34},{3,35},{4,36},{5,37},{6,38},{7,39},{8,40},{9,... | collective-permute-start | bytes 393224 | tf_op jit(solution)/shard_map/ppermute | solution.py:27
  48.4 15.5 %collective-permute-start.8 = (f32[5,1,32,2048]{3,2,1,0:T(8,128)S(1)}, f32[5,1,32,2048]{3,2,1,0:T(8,128)S(1)}, u32[]{:S(2)}, u32[]{:S(2)}) collective-permute-start(f32[5,1,32,2048]{3,2,1,0:T(8,128)S(1)} %constant_dynamic-slice_fusion.4), channel_id=1, source_target_pairs={{0,8},{1,9},{2,10},{3,11},{4,12},{5,13},{6,14},{7,15},{8,0},{9,1},... | collective-permute-start | bytes 3932168 | tf_op jit(solution)/shard_map/ppermute | solution.py:27
  53.6 7.2 %collective-permute-start.13 = (f32[32,2048]{1,0:T(8,128)S(1)}, f32[32,2048]{1,0:T(8,128)S(1)}, u32[]{:S(2)}, u32[]{:S(2)}) collective-permute-start(f32[32,2048]{1,0:T(8,128)S(1)} %get-tuple-element.42), channel_id=1, source_target_pairs={{0,32},{1,33},{2,34},{3,35},{4,36},{5,37},{6,38},{7,39},{8,40},{9,... | collective-permute-start | bytes 786440 | tf_op jit(solution)/shard_map/ppermute | solution.py:27
  54.2 9.7 %collective-permute-start.14 = (f32[32,2048]{1,0:T(8,128)S(1)}, f32[32,2048]{1,0:T(8,128)S(1)}, u32[]{:S(2)}, u32[]{:S(2)}) collective-permute-start(f32[32,2048]{1,0:T(8,128)S(1)} %get-tuple-element.43), channel_id=1, source_target_pairs={{0,224},{1,225},{2,226},{3,227},{4,228},{5,229},{6,230},{7,231},{8... | collective-permute-start | bytes 786440 | tf_op jit(solution)/shard_map/ppermute | solution.py:27
  64.2 6.6 %collective-permute-start.15 = (f32[32,2048]{1,0:T(8,128)S(1)}, f32[32,2048]{1,0:T(8,128)S(1)}, u32[]{:S(2)}, u32[]{:S(2)}) collective-permute-start(f32[32,2048]{1,0:T(8,128)S(1)} %get-tuple-element.46), channel_id=1, source_target_pairs={{0,32},{1,33},{2,34},{3,35},{4,36},{5,37},{6,38},{7,39},{8,40},{9,... | collective-permute-start | bytes 786440 | tf_op jit(solution)/shard_map/ppermute | solution.py:27
  66.0 7.0 %collective-permute-start.16 = (f32[32,2048]{1,0:T(8,128)S(1)}, f32[32,2048]{1,0:T(8,128)S(1)}, u32[]{:S(2)}, u32[]{:S(2)}) collective-permute-start(f32[32,2048]{1,0:T(8,128)S(1)} %get-tuple-element.47), channel_id=1, source_target_pairs={{0,224},{1,225},{2,226},{3,227},{4,228},{5,229},{6,230},{7,231},{8... | collective-permute-start | bytes 786440 | tf_op jit(solution)/shard_map/ppermute | solution.py:27
  73.1 6.4 %collective-permute-start.17 = (f32[32,2048]{1,0:T(8,128)S(1)}, f32[32,2048]{1,0:T(8,128)S(1)}, u32[]{:S(2)}, u32[]{:S(2)}) collective-permute-start(f32[32,2048]{1,0:T(8,128)S(1)} %get-tuple-element.50), channel_id=1, source_target_pairs={{0,32},{1,33},{2,34},{3,35},{4,36},{5,37},{6,38},{7,39},{8,40},{9,... | collective-permute-start | bytes 786440 | tf_op jit(solution)/shard_map/ppermute | solution.py:27
  75.2 6.4 %collective-permute-start.18 = (f32[32,2048]{1,0:T(8,128)S(1)}, f32[32,2048]{1,0:T(8,128)S(1)}, u32[]{:S(2)}, u32[]{:S(2)}) collective-permute-start(f32[32,2048]{1,0:T(8,128)S(1)} %get-tuple-element.51), channel_id=1, source_target_pairs={{0,224},{1,225},{2,226},{3,227},{4,228},{5,229},{6,230},{7,231},{8... | collective-permute-start | bytes 786440 | tf_op jit(solution)/shard_map/ppermute | solution.py:27
  81.6 8.0 %collective-permute-start.19 = (f32[32,2048]{1,0:T(8,128)S(1)}, f32[32,2048]{1,0:T(8,128)S(1)}, u32[]{:S(2)}, u32[]{:S(2)}) collective-permute-start(f32[32,2048]{1,0:T(8,128)S(1)} %fusion.8), channel_id=1, source_target_pairs={{0,16},{1,17},{2,18},{3,19},{4,20},{5,21},{6,22},{7,23},{8,24},{9,... | collective-permute-start | bytes 786440 | tf_op jit(solution)/shard_map/ppermute | solution.py:27
  89.6 8.7 %collective-permute-start.26 = (f32[32,2048]{1,0:T(8,128)S(1)}, f32[32,2048]{1,0:T(8,128)S(1)}, u32[]{:S(2)}, u32[]{:S(2)}) collective-permute-start(f32[32,2048]{1,0:T(8,128)S(1)} %add.201), channel_id=1, source_target_pairs={{0,32},{1,33},{2,34},{3,35},{4,36},{5,37},{6,38},{7,39},{8,40},{9,... | collective-permute-start | bytes 786440 | tf_op jit(solution)/shard_map/ppermute | solution.py:27
  91.2 8.5 %collective-permute-start.27 = (f32[32,2048]{1,0:T(8,128)S(1)}, f32[32,2048]{1,0:T(8,128)S(1)}, u32[]{:S(2)}, u32[]{:S(2)}) collective-permute-start(f32[32,2048]{1,0:T(8,128)S(1)} %add.201), channel_id=1, source_target_pairs={{0,224},{1,225},{2,226},{3,227},{4,228},{5,229},{6,230},{7,231},{8... | collective-permute-start | bytes 786440 | tf_op jit(solution)/shard_map/ppermute | solution.py:27
  99.7 7.6 %collective-permute-start.28 = (f32[32,2048]{1,0:T(8,128)S(1)}, f32[32,2048]{1,0:T(8,128)S(1)}, u32[]{:S(2)}, u32[]{:S(2)}) collective-permute-start(f32[32,2048]{1,0:T(8,128)S(1)} %collective-permute-done.26), channel_id=1, source_target_pairs={{0,32},{1,33},{2,34},{3,35},{4,36},{5,37},{6,38},{7,39},{8,40},{9,... | collective-permute-start | bytes 786440 | tf_op jit(solution)/shard_map/ppermute | solution.py:27
  101.3 7.6 %collective-permute-start.29 = (f32[32,2048]{1,0:T(8,128)S(1)}, f32[32,2048]{1,0:T(8,128)S(1)}, u32[]{:S(2)}, u32[]{:S(2)}) collective-permute-start(f32[32,2048]{1,0:T(8,128)S(1)} %collective-permute-done.27), channel_id=1, source_target_pairs={{0,224},{1,225},{2,226},{3,227},{4,228},{5,229},{6,230},{7,231},{8... | collective-permute-start | bytes 786440 | tf_op jit(solution)/shard_map/ppermute | solution.py:27
  108.9 6.6 %collective-permute-start.31 = (f32[32,2048]{1,0:T(8,128)S(1)}, f32[32,2048]{1,0:T(8,128)S(1)}, u32[]{:S(2)}, u32[]{:S(2)}) collective-permute-start(f32[32,2048]{1,0:T(8,128)S(1)} %collective-permute-done.28), channel_id=1, source_target_pairs={{0,32},{1,33},{2,34},{3,35},{4,36},{5,37},{6,38},{7,39},{8,40},{9,... | collective-permute-start | bytes 786440 | tf_op jit(solution)/shard_map/ppermute | solution.py:27
  110.6 7.3 %collective-permute-start.32 = (f32[32,2048]{1,0:T(8,128)S(1)}, f32[32,2048]{1,0:T(8,128)S(1)}, u32[]{:S(2)}, u32[]{:S(2)}) collective-permute-start(f32[32,2048]{1,0:T(8,128)S(1)} %collective-permute-done.29), channel_id=1, source_target_pairs={{0,224},{1,225},{2,226},{3,227},{4,228},{5,229},{6,230},{7,231},{8... | collective-permute-start | bytes 786440 | tf_op jit(solution)/shard_map/ppermute | solution.py:27
  111.0 42.9 %collective-permute-start.30 = (f32[128,2048]{1,0:T(8,128)S(1)}, f32[128,2048]{1,0:T(8,128)S(1)}, u32[]{:S(2)}, u32[]{:S(2)}) collective-permute-start(f32[128,2048]{1,0:T(8,128)S(1)} %pad_maximum_fusion.refs_8_), channel_id=1, source_target_pairs={{0,8},{1,9},{2,10},{3,11},{4,12},{5,13},{6,14},{7,15},{8,0},{9,1},... | collective-permute-start | bytes 3145736 | tf_op jit(solution)/shard_map/ppermute | solution.py:27
  124.7 29.2 %collective-permute-start.35 = (f32[128,2048]{1,0:T(8,128)S(1)}, f32[128,2048]{1,0:T(8,128)}, u32[]{:S(2)}, u32[]{:S(2)}) collective-permute-start(f32[128,2048]{1,0:T(8,128)S(1)} %constant_dynamic-update-slice_fusion.5.refs_10_), channel_id=1, source_target_pairs={{0,8},{1,9},{2,10},{3,11},{4,12},{5,13},{6,14},{7,15},{8,0},{9,1},... | collective-permute-start | bytes 3145736 | tf_op jit(solution)/shard_map/ppermute | solution.py:27
  124.8 7.9 %collective-permute-start.20 = (f32[32,1024]{1,0:T(8,128)S(1)}, f32[32,1024]{1,0:T(8,128)S(1)}, u32[]{:S(2)}, u32[]{:S(2)}) collective-permute-start(f32[32,1024]{1,0:T(8,128)S(1)} %constant_dynamic-slice_fusion.1), channel_id=1, source_target_pairs={{0,0},{1,33},{2,66},{3,99},{4,132},{5,165},{6,198},{7,231},{8,8},{... | collective-permute-start | bytes 393224 | tf_op jit(solution)/shard_map/ppermute | solution.py:27
  134.0 12.3 %collective-permute-start.22 = (f32[64,512]{1,0:T(8,128)S(1)}, f32[64,512]{1,0:T(8,128)}, u32[]{:S(2)}, u32[]{:S(2)}) collective-permute-start(f32[64,512]{1,0:T(8,128)S(1)} %bitcast.71), channel_id=1, source_target_pairs={{0,4},{1,5},{2,6},{3,7},{4,0},{5,1},{6,2},{7,3},{8,12},{9,13},{10,... | collective-permute-start | bytes 393224 | tf_op jit(solution)/shard_map/ppermute | solution.py:27
  147.2 13.8 %collective-permute-start.23 = (f32[128,512]{1,0:T(8,128)S(1)}, f32[128,512]{1,0:T(8,128)S(1)}, u32[]{:S(2)}, u32[]{:S(2)}) collective-permute-start(f32[128,512]{1,0:T(8,128)S(1)} %pad_maximum_fusion.1.refs_0_), channel_id=1, source_target_pairs={{0,1},{1,2},{2,3},{3,0},{4,5},{5,6},{6,7},{7,4},{8,9},{9,10},{10,1... | collective-permute-start | bytes 786440 | tf_op jit(solution)/shard_map/ppermute | solution.py:27
  147.3 15.8 %collective-permute-start.24 = (f32[128,512]{1,0:T(8,128)S(1)}, f32[128,512]{1,0:T(8,128)S(1)}, u32[]{:S(2)}, u32[]{:S(2)}) collective-permute-start(f32[128,512]{1,0:T(8,128)S(1)} %pad_maximum_fusion.1.refs_0_), channel_id=1, source_target_pairs={{0,3},{1,0},{2,1},{3,2},{4,7},{5,4},{6,5},{7,6},{8,11},{9,8},{10,9... | collective-permute-start | bytes 786440 | tf_op jit(solution)/shard_map/ppermute | solution.py:27
  152.5 12.5 %collective-permute-start.25 = (f32[128,512]{1,0:T(8,128)S(1)}, f32[128,512]{1,0:T(8,128)S(1)}, u32[]{:S(2)}, u32[]{:S(2)}) collective-permute-start(f32[128,512]{1,0:T(8,128)S(1)} %pad_maximum_fusion.1.refs_0_), channel_id=1, source_target_pairs={{0,2},{1,3},{2,0},{3,1},{4,6},{5,7},{6,4},{7,5},{8,10},{9,11},{10,... | collective-permute-start | bytes 786440 | tf_op jit(solution)/shard_map/ppermute | solution.py:27
  (14 other events, 218.0 us)

commit v2 on v1

--- a/solution.py
+++ b/solution.py
@@ -56,7 +56,7 @@
     return moved(array, lambda z, yh, core, col: (z, 1 - yh, core, col))
 
 
-LANES = 512
+LANES = 256
 
 
 def in_hbm(array):
@@ -158,14 +158,14 @@
         depth,
         rows,
         cols,
-        pltpu.HBM((rows, cols), jnp.float32),
+        jax.ShapeDtypeStruct((rows, cols), jnp.float32),
     )
 
 
 def updated(scale, offset, lefts, samples, order, addend, omega, diag):
     depth, cols = samples.shape
     rows = lefts[0].shape[1]
-    samples, addend, omega = in_hbm(samples), in_hbm(addend), in_hbm(omega)
+    samples = in_hbm(samples)
     piece_rows = depth // len(order)
 
     def piece(i):

time: 177 us -> 177 us (level)
  transfers between devices with their start and end apart: 36 -> 36, of which waited for: 27 -> 27; matrix products, arithmetic and copies ran while one was open for 6% -> 6% of each run, Pallas kernels for 4% -> 5%
where the time goes in v2:
time: 177 us; the launch traced here: 175 us
  waiting for transfers between devices  80.6 us (46%)
  starting transfers between devices  63.8 us (36%)
  Pallas kernels  17.9 us (10%)
  matrix products  5.52 us (3%)
  other arithmetic  5.02 us (3%)
    ppermute x36, waiting for transfers between devices, moved(): lax.ppermute(array, ALL, [(place(*at), place(*target(*at))) for at in eve...  80.6 us
    ppermute x36, starting transfers between devices, moved(): lax.ppermute(array, ALL, [(place(*at), place(*target(*at))) for at in eve...  63.8 us
    pallas_call x2, Pallas kernels, call(): pl.pallas_call(kernel, grid_spec=pltpu.PrefetchScalarGridSpec(num_scalar_...  17.9 us
    dot_general x3, matrix products, dot(): jnp.dot(left, right, precision=lax.Precision.HIGH, preferred_element_type...  5.52 us
  transfers between devices with their start and end apart: 36, of which 27 were waited for; matrix products, arithmetic and copies ran while one was open for 6% of the time, Pallas kernels for 5%

profile of v2, /device:TPU:32, one launch (start us, length us, event | category | flops | bytes accessed | tf_op | source)
XLA Modules:
  0.0 175.0 jit_solution(18231118158868961522)
XLA Ops:
  0.9 2.9 %collective-permute-start = (f32[64,512]{1,0:T(8,128)S(1)}, f32[64,512]{1,0:T(8,128)S(1)}, u32[]{:S(2)}, u32[]{:S(2)}) collective-permute-start(f32[64,512]{1,0:T(8,128)S(1)} %dynamic_slice.33), channel_id=1, source_target_pairs={{0,0},{1,33},{2,66},{3,99},{4,132},{5,165},{6,198},{7,231},{8,8},{... | collective-permute-start | bytes 393224 | tf_op jit(solution)/shard_map/ppermute | solution.py:27
  4.8 2.7 %fusion.refs_13_ = f32[512,2048]{1,0:T(8,128)S(1)} fusion(f32[512,2048]{1,0:T(8,128)} %param.5, f32[2,2048]{1,0:T(2,128)S(1)} %bitcast.73, f32[512]{0:T(512)} %param.6, s32[2048]{0:T(1024)S(1)} %iota_add_fusion, s32[512]{0:T(512)S(1)} %iota_add_fusion.1), kind=kLoop, calls=%fused_computation.1 | loop fusion | flops 3145728 | bytes 8417280 | tf_op jit(solution)/shard_map/jit(_where)/select_n | solution.py:234
  9.5 12.6 %collective-permute-start.2 = (f32[64,512]{1,0:T(8,128)S(1)}, f32[64,512]{1,0:T(8,128)S(1)}, u32[]{:S(2)}, u32[]{:S(2)}) collective-permute-start(f32[64,512]{1,0:T(8,128)S(1)} %collective-permute-done.refs_7_), channel_id=1, source_target_pairs={{0,1},{1,0},{2,3},{3,2},{4,5},{5,4},{6,7},{7,6},{8,9},{9,8},{10,11... | collective-permute-start | bytes 393224 | tf_op jit(solution)/shard_map/ppermute | solution.py:27
  25.5 2.4 %collective-permute-start.3 = (f32[64,512]{1,0:T(8,128)S(1)}, f32[64,512]{1,0:T(8,128)S(1)}, u32[]{:S(2)}, u32[]{:S(2)}) collective-permute-start(f32[64,512]{1,0:T(8,128)S(1)} %collective-permute-done.refs_7_), channel_id=1, source_target_pairs={{0,6},{1,7},{2,4},{3,5},{4,2},{5,3},{6,0},{7,1},{8,14},{9,15},{10,... | collective-permute-start | bytes 393224 | tf_op jit(solution)/shard_map/ppermute | solution.py:27
  28.6 4.3 %collective-permute-start.5 = (f32[64,512]{1,0:T(8,128)S(1)}, f32[64,512]{1,0:T(8,128)S(1)}, u32[]{:S(2)}, u32[]{:S(2)}) collective-permute-start(f32[64,512]{1,0:T(8,128)S(1)} %collective-permute-done.refs_7_), channel_id=1, source_target_pairs={{0,5},{1,4},{2,7},{3,6},{4,1},{5,0},{6,3},{7,2},{8,13},{9,12},{10,... | collective-permute-start | bytes 393224 | tf_op jit(solution)/shard_map/ppermute | solution.py:27
  36.4 3.2 %collective-permute-done.5.refs_1_ = f32[64,512]{1,0:T(8,128)S(1)} collective-permute-done((f32[64,512]{1,0:T(8,128)S(1)}, f32[64,512]{1,0:T(8,128)S(1)}, u32[]{:S(2)}, u32[]{:S(2)}) %collective-permute-start.5) | collective-permute-done | bytes 131104 | tf_op jit(solution)/shard_map/ppermute | solution.py:27
  40.0 2.7 %collective-permute-done.7.refs_0_ = f32[64,512]{1,0:T(8,128)S(1)} collective-permute-done((f32[64,512]{1,0:T(8,128)S(1)}, f32[64,512]{1,0:T(8,128)S(1)}, u32[]{:S(2)}, u32[]{:S(2)}) %collective-permute-start.7) | collective-permute-done | bytes 131104 | tf_op jit(solution)/shard_map/ppermute | solution.py:27
  42.7 2.5 %fusion.14 = f32[320,2048]{1,0:T(8,128)S(1)} fusion(f32[320,512]{1,0:T(8,128)S(1)} %constant_dynamic-update-slice_fusion, f32[512,2048]{1,0:T(8,128)S(1)} %fusion.refs_13_), kind=kOutput, calls=%fused_computation.50 | convolution fusion | flops 2013265920 | bytes 7471104 | tf_op jit(solution)/shard_map/dot_general | solution.py:78
  45.3 3.0 %collective-permute-start.11 = (f32[16,2048]{1,0:T(8,128)S(1)}, f32[16,2048]{1,0:T(8,128)S(1)}, u32[]{:S(2)}, u32[]{:S(2)}) collective-permute-start(f32[16,2048]{1,0:T(8,128)S(1)} %get-tuple-element.38), channel_id=1, source_target_pairs={{0,32},{1,33},{2,34},{3,35},{4,36},{5,37},{6,38},{7,39},{8,40},{9,... | collective-permute-start | bytes 393224 | tf_op jit(solution)/shard_map/ppermute | solution.py:27
  48.5 2.7 %collective-permute-done.11 = f32[16,2048]{1,0:T(8,128)S(1)} collective-permute-done((f32[16,2048]{1,0:T(8,128)S(1)}, f32[16,2048]{1,0:T(8,128)S(1)}, u32[]{:S(2)}, u32[]{:S(2)}) %collective-permute-start.11) | collective-permute-done | bytes 131104 | tf_op jit(solution)/shard_map/ppermute | solution.py:27
  51.2 2.2 %collective-permute-done.12 = f32[16,2048]{1,0:T(8,128)S(1)} collective-permute-done((f32[16,2048]{1,0:T(8,128)S(1)}, f32[16,2048]{1,0:T(8,128)S(1)}, u32[]{:S(2)}, u32[]{:S(2)}) %collective-permute-start.12) | collective-permute-done | bytes 131104 | tf_op jit(solution)/shard_map/ppermute | solution.py:27
  55.7 5.1 %collective-permute-done.13 = f32[32,2048]{1,0:T(8,128)S(1)} collective-permute-done((f32[32,2048]{1,0:T(8,128)S(1)}, f32[32,2048]{1,0:T(8,128)S(1)}, u32[]{:S(2)}, u32[]{:S(2)}) %collective-permute-start.13) | collective-permute-done | bytes 262176 | tf_op jit(solution)/shard_map/ppermute | solution.py:27
  60.7 3.2 %collective-permute-done.14 = f32[32,2048]{1,0:T(8,128)S(1)} collective-permute-done((f32[32,2048]{1,0:T(8,128)S(1)}, f32[32,2048]{1,0:T(8,128)S(1)}, u32[]{:S(2)}, u32[]{:S(2)}) %collective-permute-start.14) | collective-permute-done | bytes 262176 | tf_op jit(solution)/shard_map/ppermute | solution.py:27
  66.3 4.5 %collective-permute-done.15 = f32[32,2048]{1,0:T(8,128)S(1)} collective-permute-done((f32[32,2048]{1,0:T(8,128)S(1)}, f32[32,2048]{1,0:T(8,128)S(1)}, u32[]{:S(2)}, u32[]{:S(2)}) %collective-permute-start.15) | collective-permute-done | bytes 262176 | tf_op jit(solution)/shard_map/ppermute | solution.py:27
  70.8 2.3 %collective-permute-done.16 = f32[32,2048]{1,0:T(8,128)S(1)} collective-permute-done((f32[32,2048]{1,0:T(8,128)S(1)}, f32[32,2048]{1,0:T(8,128)S(1)}, u32[]{:S(2)}, u32[]{:S(2)}) %collective-permute-start.16) | collective-permute-done | bytes 262176 | tf_op jit(solution)/shard_map/ppermute | solution.py:27
  73.1 2.1 %collective-permute-start.17 = (f32[32,2048]{1,0:T(8,128)S(1)}, f32[32,2048]{1,0:T(8,128)S(1)}, u32[]{:S(2)}, u32[]{:S(2)}) collective-permute-start(f32[32,2048]{1,0:T(8,128)S(1)} %get-tuple-element.50), channel_id=1, source_target_pairs={{0,32},{1,33},{2,34},{3,35},{4,36},{5,37},{6,38},{7,39},{8,40},{9,... | collective-permute-start | bytes 786440 | tf_op jit(solution)/shard_map/ppermute | solution.py:27
  75.2 4.3 %collective-permute-done.17 = f32[32,2048]{1,0:T(8,128)S(1)} collective-permute-done((f32[32,2048]{1,0:T(8,128)S(1)}, f32[32,2048]{1,0:T(8,128)S(1)}, u32[]{:S(2)}, u32[]{:S(2)}) %collective-permute-start.17) | collective-permute-done | bytes 262176 | tf_op jit(solution)/shard_map/ppermute | solution.py:27
  79.5 2.0 %collective-permute-done.18 = f32[32,2048]{1,0:T(8,128)S(1)} collective-permute-done((f32[32,2048]{1,0:T(8,128)S(1)}, f32[32,2048]{1,0:T(8,128)S(1)}, u32[]{:S(2)}, u32[]{:S(2)}) %collective-permute-start.18) | collective-permute-done | bytes 262176 | tf_op jit(solution)/shard_map/ppermute | solution.py:27
  81.6 3.2 %collective-permute-start.19 = (f32[32,2048]{1,0:T(8,128)S(1)}, f32[32,2048]{1,0:T(8,128)S(1)}, u32[]{:S(2)}, u32[]{:S(2)}) collective-permute-start(f32[32,2048]{1,0:T(8,128)S(1)} %fusion.8), channel_id=1, source_target_pairs={{0,16},{1,17},{2,18},{3,19},{4,20},{5,21},{6,22},{7,23},{8,24},{9,... | collective-permute-start | bytes 786440 | tf_op jit(solution)/shard_map/ppermute | solution.py:27
  84.8 4.8 %collective-permute-done.19 = f32[32,2048]{1,0:T(8,128)S(1)} collective-permute-done((f32[32,2048]{1,0:T(8,128)S(1)}, f32[32,2048]{1,0:T(8,128)S(1)}, u32[]{:S(2)}, u32[]{:S(2)}) %collective-permute-start.19) | collective-permute-done | bytes 262176 | tf_op jit(solution)/shard_map/ppermute | solution.py:27
  91.7 6.6 %collective-permute-done.26 = f32[32,2048]{1,0:T(8,128)S(1)} collective-permute-done((f32[32,2048]{1,0:T(8,128)S(1)}, f32[32,2048]{1,0:T(8,128)S(1)}, u32[]{:S(2)}, u32[]{:S(2)}) %collective-permute-start.26) | collective-permute-done | bytes 262176 | tf_op jit(solution)/shard_map/ppermute | solution.py:27
  101.7 5.6 %collective-permute-done.28 = f32[32,2048]{1,0:T(8,128)S(1)} collective-permute-done((f32[32,2048]{1,0:T(8,128)S(1)}, f32[32,2048]{1,0:T(8,128)S(1)}, u32[]{:S(2)}, u32[]{:S(2)}) %collective-permute-start.28) | collective-permute-done | bytes 262176 | tf_op jit(solution)/shard_map/ppermute | solution.py:27
  111.1 4.4 %collective-permute-done.31 = f32[32,2048]{1,0:T(8,128)S(1)} collective-permute-done((f32[32,2048]{1,0:T(8,128)S(1)}, f32[32,2048]{1,0:T(8,128)S(1)}, u32[]{:S(2)}, u32[]{:S(2)}) %collective-permute-start.31) | collective-permute-done | bytes 262176 | tf_op jit(solution)/shard_map/ppermute | solution.py:27
  115.5 2.4 %collective-permute-done.32 = f32[32,2048]{1,0:T(8,128)S(1)} collective-permute-done((f32[32,2048]{1,0:T(8,128)S(1)}, f32[32,2048]{1,0:T(8,128)S(1)}, u32[]{:S(2)}, u32[]{:S(2)}) %collective-permute-start.32) | collective-permute-done | bytes 262176 | tf_op jit(solution)/shard_map/ppermute | solution.py:27
  120.3 2.8 %collective-permute-done.33 = f32[16,2048]{1,0:T(8,128)S(1)} collective-permute-done((f32[16,2048]{1,0:T(8,128)S(1)}, f32[16,2048]{1,0:T(8,128)S(1)}, u32[]{:S(2)}, u32[]{:S(2)}) %collective-permute-start.33) | collective-permute-done | bytes 131104 | tf_op jit(solution)/shard_map/ppermute | solution.py:27
  124.8 1.9 %collective-permute-start.20 = (f32[32,1024]{1,0:T(8,128)S(1)}, f32[32,1024]{1,0:T(8,128)S(1)}, u32[]{:S(2)}, u32[]{:S(2)}) collective-permute-start(f32[32,1024]{1,0:T(8,128)S(1)} %constant_dynamic-slice_fusion.1), channel_id=1, source_target_pairs={{0,0},{1,33},{2,66},{3,99},{4,132},{5,165},{6,198},{7,231},{8,8},{... | collective-permute-start | bytes 393224 | tf_op jit(solution)/shard_map/ppermute | solution.py:27
  126.8 5.9 %collective-permute-done.20 = f32[32,1024]{1,0:T(8,128)S(1)} collective-permute-done((f32[32,1024]{1,0:T(8,128)S(1)}, f32[32,1024]{1,0:T(8,128)S(1)}, u32[]{:S(2)}, u32[]{:S(2)}) %collective-permute-start.20) | collective-permute-done | bytes 131104 | tf_op jit(solution)/shard_map/ppermute | solution.py:27
  134.0 8.4 %collective-permute-start.22 = (f32[64,512]{1,0:T(8,128)S(1)}, f32[64,512]{1,0:T(8,128)}, u32[]{:S(2)}, u32[]{:S(2)}) collective-permute-start(f32[64,512]{1,0:T(8,128)S(1)} %bitcast.71), channel_id=1, source_target_pairs={{0,4},{1,5},{2,6},{3,7},{4,0},{5,1},{6,2},{7,3},{8,12},{9,13},{10,... | collective-permute-start | bytes 393224 | tf_op jit(solution)/shard_map/ppermute | solution.py:27
  142.6 3.7 %collective-permute-done.22 = f32[64,512]{1,0:T(8,128)} collective-permute-done((f32[64,512]{1,0:T(8,128)S(1)}, f32[64,512]{1,0:T(8,128)}, u32[]{:S(2)}, u32[]{:S(2)}) %collective-permute-start.22) | collective-permute-done | bytes 131104 | tf_op jit(solution)/shard_map/ppermute | solution.py:27
  147.3 5.2 %collective-permute-start.24 = (f32[128,512]{1,0:T(8,128)S(1)}, f32[128,512]{1,0:T(8,128)S(1)}, u32[]{:S(2)}, u32[]{:S(2)}) collective-permute-start(f32[128,512]{1,0:T(8,128)S(1)} %pad_maximum_fusion.1.refs_0_), channel_id=1, source_target_pairs={{0,3},{1,0},{2,1},{3,2},{4,7},{5,4},{6,5},{7,6},{8,11},{9,8},{10,9... | collective-permute-start | bytes 786440 | tf_op jit(solution)/shard_map/ppermute | solution.py:27
  153.9 7.9 %shard_map.46.refs_12_ = f32[512,2048]{1,0:T(8,128)S(1)} custom-call(s32[1]{0:T(128)} %bitcast.25.core, f32[64,512]{1,0:T(8,128)} %copy-done.9, f32[64,512]{1,0:T(8,128)} %copy-done.7, f32[64,512]{1,0:T(8,128)} %copy-done.8, f32[64,512]{1,0:T(8,128)} %copy-done.5, f32[64,512]{1,0:T(8,128)} %copy-done.6, f32[64,512]{1,0:T(8,128)} %copy-done.3, ...), custom_call_target="tpu_custom_call" | custom-call | flops 3221225472 | bytes 13631488 | tf_op jit(solution)/shard_map/pallas_call | solution.py:130
  165.0 10.0 %shard_map.47 = f32[512,2048]{1,0:T(8,128)} custom-call(s32[9]{0:T(128)S(1)} %stack.39.at, f32[128,512]{1,0:T(8,128)S(1)} %pad_maximum_fusion.1.refs_0_, f32[128,512]{1,0:T(8,128)S(1)} %collective-permute-done.23.refs_1_, f32[128,512]{1,0:T(8,128)S(1)} %collective-permute-done.24.refs_2_, f32[128,512]{1,0:T(8,128)S(1)} %collective-permute-done.25.refs_3_, ...), custom_call_target="tpu_custom_call" | custom-call | flops 3221225472 | bytes 13631488 | tf_op jit(solution)/shard_map/pallas_call | solution.py:130
  (107 shorter events, 36.9 us)
Async XLA Ops:
  0.9 7.9 %collective-permute-start = (f32[64,512]{1,0:T(8,128)S(1)}, f32[64,512]{1,0:T(8,128)S(1)}, u32[]{:S(2)}, u32[]{:S(2)}) collective-permute-start(f32[64,512]{1,0:T(8,128)S(1)} %dynamic_slice.33), channel_id=1, source_target_pairs={{0,0},{1,33},{2,66},{3,99},{4,132},{5,165},{6,198},{7,231},{8,8},{... | collective-permute-start | bytes 393224 | tf_op jit(solution)/shard_map/ppermute | solution.py:27
  8.8 15.0 %collective-permute-start.1 = (f32[64,512]{1,0:T(8,128)S(1)}, f32[64,512]{1,0:T(8,128)S(1)}, u32[]{:S(2)}, u32[]{:S(2)}) collective-permute-start(f32[64,512]{1,0:T(8,128)S(1)} %collective-permute-done.refs_7_), channel_id=1, source_target_pairs={{0,7},{1,6},{2,5},{3,4},{4,3},{5,2},{6,1},{7,0},{8,15},{9,14},{10,... | collective-permute-start | bytes 393224 | tf_op jit(solution)/shard_map/ppermute | solution.py:27
  9.5 16.0 %collective-permute-start.2 = (f32[64,512]{1,0:T(8,128)S(1)}, f32[64,512]{1,0:T(8,128)S(1)}, u32[]{:S(2)}, u32[]{:S(2)}) collective-permute-start(f32[64,512]{1,0:T(8,128)S(1)} %collective-permute-done.refs_7_), channel_id=1, source_target_pairs={{0,1},{1,0},{2,3},{3,2},{4,5},{5,4},{6,7},{7,6},{8,9},{9,8},{10,11... | collective-permute-start | bytes 393224 | tf_op jit(solution)/shard_map/ppermute | solution.py:27
  23.7 10.8 %collective-permute-start.10 = (f32[1,1,32,2048]{3,2,1,0:T(8,128)S(1)}, f32[1,1,32,2048]{3,2,1,0:T(8,128)S(1)}, u32[]{:S(2)}, u32[]{:S(2)}) collective-permute-start(f32[1,1,32,2048]{3,2,1,0:T(8,128)S(1)} %constant_dynamic-slice_fusion.2), channel_id=1, source_target_pairs={{0,8},{1,9},{2,10},{3,11},{4,12},{5,13},{6,14},{7,15},{8,0},{9,1},... | collective-permute-start | bytes 786440 | tf_op jit(solution)/shard_map/ppermute | solution.py:27
  25.5 10.7 %collective-permute-start.3 = (f32[64,512]{1,0:T(8,128)S(1)}, f32[64,512]{1,0:T(8,128)S(1)}, u32[]{:S(2)}, u32[]{:S(2)}) collective-permute-start(f32[64,512]{1,0:T(8,128)S(1)} %collective-permute-done.refs_7_), channel_id=1, source_target_pairs={{0,6},{1,7},{2,4},{3,5},{4,2},{5,3},{6,0},{7,1},{8,14},{9,15},{10,... | collective-permute-start | bytes 393224 | tf_op jit(solution)/shard_map/ppermute | solution.py:27
  27.9 8.4 %collective-permute-start.4 = (f32[64,512]{1,0:T(8,128)S(1)}, f32[64,512]{1,0:T(8,128)S(1)}, u32[]{:S(2)}, u32[]{:S(2)}) collective-permute-start(f32[64,512]{1,0:T(8,128)S(1)} %collective-permute-done.refs_7_), channel_id=1, source_target_pairs={{0,2},{1,3},{2,0},{3,1},{4,6},{5,7},{6,4},{7,5},{8,10},{9,11},{10,... | collective-permute-start | bytes 393224 | tf_op jit(solution)/shard_map/ppermute | solution.py:27
  28.6 11.0 %collective-permute-start.5 = (f32[64,512]{1,0:T(8,128)S(1)}, f32[64,512]{1,0:T(8,128)S(1)}, u32[]{:S(2)}, u32[]{:S(2)}) collective-permute-start(f32[64,512]{1,0:T(8,128)S(1)} %collective-permute-done.refs_7_), channel_id=1, source_target_pairs={{0,5},{1,4},{2,7},{3,6},{4,1},{5,0},{6,3},{7,2},{8,13},{9,12},{10,... | collective-permute-start | bytes 393224 | tf_op jit(solution)/shard_map/ppermute | solution.py:27
  32.9 7.1 %collective-permute-start.6 = (f32[64,512]{1,0:T(8,128)S(1)}, f32[64,512]{1,0:T(8,128)S(1)}, u32[]{:S(2)}, u32[]{:S(2)}) collective-permute-start(f32[64,512]{1,0:T(8,128)S(1)} %collective-permute-done.refs_7_), channel_id=1, source_target_pairs={{0,3},{1,2},{2,1},{3,0},{4,7},{5,6},{6,5},{7,4},{8,11},{9,10},{10,... | collective-permute-start | bytes 393224 | tf_op jit(solution)/shard_map/ppermute | solution.py:27
  34.5 8.2 %collective-permute-start.7 = (f32[64,512]{1,0:T(8,128)S(1)}, f32[64,512]{1,0:T(8,128)S(1)}, u32[]{:S(2)}, u32[]{:S(2)}) collective-permute-start(f32[64,512]{1,0:T(8,128)S(1)} %collective-permute-done.refs_7_), channel_id=1, source_target_pairs={{0,4},{1,5},{2,6},{3,7},{4,0},{5,1},{6,2},{7,3},{8,12},{9,13},{10,... | collective-permute-start | bytes 393224 | tf_op jit(solution)/shard_map/ppermute | solution.py:27
  36.2 17.2 %collective-permute-start.9 = (f32[2,1,32,2048]{3,2,1,0:T(8,128)S(1)}, f32[2,1,32,2048]{3,2,1,0:T(8,128)S(1)}, u32[]{:S(2)}, u32[]{:S(2)}) collective-permute-start(f32[2,1,32,2048]{3,2,1,0:T(8,128)S(1)} %constant_dynamic-slice_fusion.3), channel_id=1, source_target_pairs={{0,8},{1,9},{2,10},{3,11},{4,12},{5,13},{6,14},{7,15},{8,0},{9,1},... | collective-permute-start | bytes 1572872 | tf_op jit(solution)/shard_map/ppermute | solution.py:27
  45.3 5.9 %collective-permute-start.11 = (f32[16,2048]{1,0:T(8,128)S(1)}, f32[16,2048]{1,0:T(8,128)S(1)}, u32[]{:S(2)}, u32[]{:S(2)}) collective-permute-start(f32[16,2048]{1,0:T(8,128)S(1)} %get-tuple-element.38), channel_id=1, source_target_pairs={{0,32},{1,33},{2,34},{3,35},{4,36},{5,37},{6,38},{7,39},{8,40},{9,... | collective-permute-start | bytes 393224 | tf_op jit(solution)/shard_map/ppermute | solution.py:27
  48.4 15.5 %collective-permute-start.8 = (f32[5,1,32,2048]{3,2,1,0:T(8,128)S(1)}, f32[5,1,32,2048]{3,2,1,0:T(8,128)S(1)}, u32[]{:S(2)}, u32[]{:S(2)}) collective-permute-start(f32[5,1,32,2048]{3,2,1,0:T(8,128)S(1)} %constant_dynamic-slice_fusion.4), channel_id=1, source_target_pairs={{0,8},{1,9},{2,10},{3,11},{4,12},{5,13},{6,14},{7,15},{8,0},{9,1},... | collective-permute-start | bytes 3932168 | tf_op jit(solution)/shard_map/ppermute | solution.py:27
  53.6 7.2 %collective-permute-start.13 = (f32[32,2048]{1,0:T(8,128)S(1)}, f32[32,2048]{1,0:T(8,128)S(1)}, u32[]{:S(2)}, u32[]{:S(2)}) collective-permute-start(f32[32,2048]{1,0:T(8,128)S(1)} %get-tuple-element.42), channel_id=1, source_target_pairs={{0,32},{1,33},{2,34},{3,35},{4,36},{5,37},{6,38},{7,39},{8,40},{9,... | collective-permute-start | bytes 786440 | tf_op jit(solution)/shard_map/ppermute | solution.py:27
  54.2 9.7 %collective-permute-start.14 = (f32[32,2048]{1,0:T(8,128)S(1)}, f32[32,2048]{1,0:T(8,128)S(1)}, u32[]{:S(2)}, u32[]{:S(2)}) collective-permute-start(f32[32,2048]{1,0:T(8,128)S(1)} %get-tuple-element.43), channel_id=1, source_target_pairs={{0,224},{1,225},{2,226},{3,227},{4,228},{5,229},{6,230},{7,231},{8... | collective-permute-start | bytes 786440 | tf_op jit(solution)/shard_map/ppermute | solution.py:27
  64.2 6.6 %collective-permute-start.15 = (f32[32,2048]{1,0:T(8,128)S(1)}, f32[32,2048]{1,0:T(8,128)S(1)}, u32[]{:S(2)}, u32[]{:S(2)}) collective-permute-start(f32[32,2048]{1,0:T(8,128)S(1)} %get-tuple-element.46), channel_id=1, source_target_pairs={{0,32},{1,33},{2,34},{3,35},{4,36},{5,37},{6,38},{7,39},{8,40},{9,... | collective-permute-start | bytes 786440 | tf_op jit(solution)/shard_map/ppermute | solution.py:27
  66.0 7.0 %collective-permute-start.16 = (f32[32,2048]{1,0:T(8,128)S(1)}, f32[32,2048]{1,0:T(8,128)S(1)}, u32[]{:S(2)}, u32[]{:S(2)}) collective-permute-start(f32[32,2048]{1,0:T(8,128)S(1)} %get-tuple-element.47), channel_id=1, source_target_pairs={{0,224},{1,225},{2,226},{3,227},{4,228},{5,229},{6,230},{7,231},{8... | collective-permute-start | bytes 786440 | tf_op jit(solution)/shard_map/ppermute | solution.py:27
  73.1 6.4 %collective-permute-start.17 = (f32[32,2048]{1,0:T(8,128)S(1)}, f32[32,2048]{1,0:T(8,128)S(1)}, u32[]{:S(2)}, u32[]{:S(2)}) collective-permute-start(f32[32,2048]{1,0:T(8,128)S(1)} %get-tuple-element.50), channel_id=1, source_target_pairs={{0,32},{1,33},{2,34},{3,35},{4,36},{5,37},{6,38},{7,39},{8,40},{9,... | collective-permute-start | bytes 786440 | tf_op jit(solution)/shard_map/ppermute | solution.py:27
  75.2 6.4 %collective-permute-start.18 = (f32[32,2048]{1,0:T(8,128)S(1)}, f32[32,2048]{1,0:T(8,128)S(1)}, u32[]{:S(2)}, u32[]{:S(2)}) collective-permute-start(f32[32,2048]{1,0:T(8,128)S(1)} %get-tuple-element.51), channel_id=1, source_target_pairs={{0,224},{1,225},{2,226},{3,227},{4,228},{5,229},{6,230},{7,231},{8... | collective-permute-start | bytes 786440 | tf_op jit(solution)/shard_map/ppermute | solution.py:27
  81.6 8.0 %collective-permute-start.19 = (f32[32,2048]{1,0:T(8,128)S(1)}, f32[32,2048]{1,0:T(8,128)S(1)}, u32[]{:S(2)}, u32[]{:S(2)}) collective-permute-start(f32[32,2048]{1,0:T(8,128)S(1)} %fusion.8), channel_id=1, source_target_pairs={{0,16},{1,17},{2,18},{3,19},{4,20},{5,21},{6,22},{7,23},{8,24},{9,... | collective-permute-start | bytes 786440 | tf_op jit(solution)/shard_map/ppermute | solution.py:27
  89.6 8.7 %collective-permute-start.26 = (f32[32,2048]{1,0:T(8,128)S(1)}, f32[32,2048]{1,0:T(8,128)S(1)}, u32[]{:S(2)}, u32[]{:S(2)}) collective-permute-start(f32[32,2048]{1,0:T(8,128)S(1)} %add.201), channel_id=1, source_target_pairs={{0,32},{1,33},{2,34},{3,35},{4,36},{5,37},{6,38},{7,39},{8,40},{9,... | collective-permute-start | bytes 786440 | tf_op jit(solution)/shard_map/ppermute | solution.py:27
  91.2 8.5 %collective-permute-start.27 = (f32[32,2048]{1,0:T(8,128)S(1)}, f32[32,2048]{1,0:T(8,128)S(1)}, u32[]{:S(2)}, u32[]{:S(2)}) collective-permute-start(f32[32,2048]{1,0:T(8,128)S(1)} %add.201), channel_id=1, source_target_pairs={{0,224},{1,225},{2,226},{3,227},{4,228},{5,229},{6,230},{7,231},{8... | collective-permute-start | bytes 786440 | tf_op jit(solution)/shard_map/ppermute | solution.py:27
  99.7 7.6 %collective-permute-start.28 = (f32[32,2048]{1,0:T(8,128)S(1)}, f32[32,2048]{1,0:T(8,128)S(1)}, u32[]{:S(2)}, u32[]{:S(2)}) collective-permute-start(f32[32,2048]{1,0:T(8,128)S(1)} %collective-permute-done.26), channel_id=1, source_target_pairs={{0,32},{1,33},{2,34},{3,35},{4,36},{5,37},{6,38},{7,39},{8,40},{9,... | collective-permute-start | bytes 786440 | tf_op jit(solution)/shard_map/ppermute | solution.py:27
  101.3 7.6 %collective-permute-start.29 = (f32[32,2048]{1,0:T(8,128)S(1)}, f32[32,2048]{1,0:T(8,128)S(1)}, u32[]{:S(2)}, u32[]{:S(2)}) collective-permute-start(f32[32,2048]{1,0:T(8,128)S(1)} %collective-permute-done.27), channel_id=1, source_target_pairs={{0,224},{1,225},{2,226},{3,227},{4,228},{5,229},{6,230},{7,231},{8... | collective-permute-start | bytes 786440 | tf_op jit(solution)/shard_map/ppermute | solution.py:27
  108.9 6.6 %collective-permute-start.31 = (f32[32,2048]{1,0:T(8,128)S(1)}, f32[32,2048]{1,0:T(8,128)S(1)}, u32[]{:S(2)}, u32[]{:S(2)}) collective-permute-start(f32[32,2048]{1,0:T(8,128)S(1)} %collective-permute-done.28), channel_id=1, source_target_pairs={{0,32},{1,33},{2,34},{3,35},{4,36},{5,37},{6,38},{7,39},{8,40},{9,... | collective-permute-start | bytes 786440 | tf_op jit(solution)/shard_map/ppermute | solution.py:27
  110.6 7.3 %collective-permute-start.32 = (f32[32,2048]{1,0:T(8,128)S(1)}, f32[32,2048]{1,0:T(8,128)S(1)}, u32[]{:S(2)}, u32[]{:S(2)}) collective-permute-start(f32[32,2048]{1,0:T(8,128)S(1)} %collective-permute-done.29), channel_id=1, source_target_pairs={{0,224},{1,225},{2,226},{3,227},{4,228},{5,229},{6,230},{7,231},{8... | collective-permute-start | bytes 786440 | tf_op jit(solution)/shard_map/ppermute | solution.py:27
  111.0 42.9 %collective-permute-start.30 = (f32[128,2048]{1,0:T(8,128)S(1)}, f32[128,2048]{1,0:T(8,128)S(1)}, u32[]{:S(2)}, u32[]{:S(2)}) collective-permute-start(f32[128,2048]{1,0:T(8,128)S(1)} %pad_maximum_fusion.refs_8_), channel_id=1, source_target_pairs={{0,8},{1,9},{2,10},{3,11},{4,12},{5,13},{6,14},{7,15},{8,0},{9,1},... | collective-permute-start | bytes 3145736 | tf_op jit(solution)/shard_map/ppermute | solution.py:27
  124.7 29.2 %collective-permute-start.35 = (f32[128,2048]{1,0:T(8,128)S(1)}, f32[128,2048]{1,0:T(8,128)}, u32[]{:S(2)}, u32[]{:S(2)}) collective-permute-start(f32[128,2048]{1,0:T(8,128)S(1)} %constant_dynamic-update-slice_fusion.5.refs_10_), channel_id=1, source_target_pairs={{0,8},{1,9},{2,10},{3,11},{4,12},{5,13},{6,14},{7,15},{8,0},{9,1},... | collective-permute-start | bytes 3145736 | tf_op jit(solution)/shard_map/ppermute | solution.py:27
  124.8 7.9 %collective-permute-start.20 = (f32[32,1024]{1,0:T(8,128)S(1)}, f32[32,1024]{1,0:T(8,128)S(1)}, u32[]{:S(2)}, u32[]{:S(2)}) collective-permute-start(f32[32,1024]{1,0:T(8,128)S(1)} %constant_dynamic-slice_fusion.1), channel_id=1, source_target_pairs={{0,0},{1,33},{2,66},{3,99},{4,132},{5,165},{6,198},{7,231},{8,8},{... | collective-permute-start | bytes 393224 | tf_op jit(solution)/shard_map/ppermute | solution.py:27
  134.0 12.3 %collective-permute-start.22 = (f32[64,512]{1,0:T(8,128)S(1)}, f32[64,512]{1,0:T(8,128)}, u32[]{:S(2)}, u32[]{:S(2)}) collective-permute-start(f32[64,512]{1,0:T(8,128)S(1)} %bitcast.71), channel_id=1, source_target_pairs={{0,4},{1,5},{2,6},{3,7},{4,0},{5,1},{6,2},{7,3},{8,12},{9,13},{10,... | collective-permute-start | bytes 393224 | tf_op jit(solution)/shard_map/ppermute | solution.py:27
  147.2 14.6 %collective-permute-start.23 = (f32[128,512]{1,0:T(8,128)S(1)}, f32[128,512]{1,0:T(8,128)S(1)}, u32[]{:S(2)}, u32[]{:S(2)}) collective-permute-start(f32[128,512]{1,0:T(8,128)S(1)} %pad_maximum_fusion.1.refs_0_), channel_id=1, source_target_pairs={{0,1},{1,2},{2,3},{3,0},{4,5},{5,6},{6,7},{7,4},{8,9},{9,10},{10,1... | collective-permute-start | bytes 786440 | tf_op jit(solution)/shard_map/ppermute | solution.py:27
  147.3 15.8 %collective-permute-start.24 = (f32[128,512]{1,0:T(8,128)S(1)}, f32[128,512]{1,0:T(8,128)S(1)}, u32[]{:S(2)}, u32[]{:S(2)}) collective-permute-start(f32[128,512]{1,0:T(8,128)S(1)} %pad_maximum_fusion.1.refs_0_), channel_id=1, source_target_pairs={{0,3},{1,0},{2,1},{3,2},{4,7},{5,4},{6,5},{7,6},{8,11},{9,8},{10,9... | collective-permute-start | bytes 786440 | tf_op jit(solution)/shard_map/ppermute | solution.py:27
  152.5 12.5 %collective-permute-start.25 = (f32[128,512]{1,0:T(8,128)S(1)}, f32[128,512]{1,0:T(8,128)S(1)}, u32[]{:S(2)}, u32[]{:S(2)}) collective-permute-start(f32[128,512]{1,0:T(8,128)S(1)} %pad_maximum_fusion.1.refs_0_), channel_id=1, source_target_pairs={{0,2},{1,3},{2,0},{3,1},{4,6},{5,7},{6,4},{7,5},{8,10},{9,11},{10,... | collective-permute-start | bytes 786440 | tf_op jit(solution)/shard_map/ppermute | solution.py:27
  (15 other events, 229.1 us)
